TPU v7x, 32 devices: a whole 2x2x4 slice. The times are simulated.
32 devices in a mesh: region: 4 (over x, core), sector: 8 (over z, y).
Axes of the slice: x: 2, y: 2, z: 4, core: 2. Of those that a mesh axis runs over, the one named last changes fastest.
Arguments:
- env_left: bfloat16 [4, 8, 2048, 2048], P('region', None, 'sector'), may hold values from -6 to 6
- site_tensor: bfloat16 [4, 2048, 2, 2048], P('region', 'sector'), may hold values from -0.125 to 0.125
- mpo_tensor: float32 [4, 8, 8, 2, 2], P('region'), may hold values from -1 to 1
- env_right: bfloat16 [4, 8, 2048, 2048], P('region', None, 'sector'), may hold values from -0.046875 to 0.046875
- bond_tensor: bfloat16 [4, 2048, 2048], P('region'), may hold values from -0.125 to 0.125
Outputs:
- env_next: bfloat16 [4, 8, 2048, 2048], P('region', None, 'sector')
- bond_image: bfloat16 [4, 2048, 2048], P('region', 'sector')
All inputs are finite; a program needn't handle non-finite values.
Results may differ from a plain program's by a relative error of at most 0.0065.
Values may be sent and summed in bfloat16 or wider, within the bound.
A program may use at most 192 MiB of HBM per device.

v0:
```python
import functools

import jax
import jax.numpy as jnp
from jax import lax
from jax.experimental import pallas as pl
from jax.experimental.pallas import tpu as pltpu
from jax.sharding import PartitionSpec as P


GROUP = 16
LANES = 128
CHUNKS = 2
SHIFTS = 4
VMEM_LIMIT = 60 * 1024 * 1024


def shifted(block, axis, distance):
    devices = range(lax.axis_size(axis))
    route = [((i - distance) % len(devices), i) for i in devices]
    return lax.ppermute(block, axis, route)


def swap(blocks):
    return lax.all_to_all(blocks, "sector", split_axis=0, concat_axis=0, tiled=True)


MESH = pl.DeviceIdType.MESH


def carried_body(mix_ref, env_ref, site_ref, *out_refs):
    width, rows, bond = env_ref.shape
    _, states, _, columns = site_ref.shape
    mix = mix_ref[...]
    mix_high = mix.astype(jnp.bfloat16)
    mix_low = (mix - mix_high.astype(jnp.float32)).astype(jnp.bfloat16)
    env = env_ref[...].reshape(width * rows, bond)
    half_done = [
        jnp.dot(env, site_ref[:, t].reshape(bond, columns), preferred_element_type=jnp.float32)
        .reshape(width, rows, columns)
        for t in range(states)
    ]
    dot = functools.partial(jnp.dot, preferred_element_type=jnp.float32)
    for g in range(rows // GROUP):
        span = slice(g * GROUP, (g + 1) * GROUP)
        x = jnp.concatenate(
            [h[:, span].reshape(width * GROUP, columns) for h in half_done], axis=0
        )
        high = x.astype(jnp.bfloat16)
        low = (x - high.astype(jnp.float32)).astype(jnp.bfloat16)
        y = dot(mix_high, high) + dot(mix_high, low) + dot(mix_low, high)
        y = y.astype(jnp.bfloat16).reshape(width, states, GROUP, columns)
        step = width // len(out_refs)
        for i, out_ref in enumerate(out_refs):
            out_ref[0, :, :, span, :] = y[i * step : (i + 1) * step]


def head_kernel(
    mix_ref, right_hbm, site_hbm, bond_hbm, left_hbm,
    gathered, moved, *rest,
):
    carried = rest[:CHUNKS]
    (right, bond_ref, blocks, own_site, shift_send, shift_recv, site_send, site_recv,
     block_send, block_recv, local_sem) = rest[CHUNKS:]
    parts, states, depth, bond = gathered.shape
    width, rows, _ = right_hbm.shape
    columns = bond // parts
    line = parts // 2
    me = lax.axis_index("sector")
    z, y = me // 2, lax.rem(me, 2)
    regions = lax.axis_size("region")
    region = lax.axis_index("region")
    before = lax.rem(region + regions - 1, regions)
    after = lax.rem(region + 1, regions)
    part_rows = rows // SHIFTS
    twin = 2 * z + 1 - y

    barrier = pltpu.get_barrier_semaphore()
    for d in range(1, parts):
        pl.semaphore_signal(
            barrier, inc=1, device_id={"sector": lax.rem(me + d, parts)}, device_id_type=MESH
        )
    for other in (before, after):
        pl.semaphore_signal(barrier, inc=1, device_id={"region": other}, device_id_type=MESH)
    pl.semaphore_wait(barrier, parts + 1)

    def shift(q):
        span = pl.ds(q * part_rows, part_rows)
        return pltpu.make_async_remote_copy(
            src_ref=right_hbm.at[:, span],
            dst_ref=right.at[:, span],
            send_sem=shift_send.at[q],
            recv_sem=shift_recv.at[q],
            device_id={"region": before},
            device_id_type=MESH,
        )

    def hop(way, source, piece, target, first=False):
        return pltpu.make_async_remote_copy(
            src_ref=site_hbm.at[piece] if first else gathered.at[source, piece],
            dst_ref=gathered.at[source, piece],
            send_sem=site_send.at[way, source, piece],
            recv_sem=site_recv.at[source, piece],
            device_id={"sector": target},
            device_id_type=MESH,
        )

    def outward(source, piece, first, ways, act):
        for way in ways:
            there = {0: me + 2, 1: me - 2, 2: twin}[way]
            if way == 2:
                act(hop(way, source, piece, there, first))
            else:
                inside = z + 1 < line if way == 0 else z >= 1

                @pl.when(inside)
                def _():
                    act(hop(way, source, piece, there, first))

    def block(q, d):
        return pltpu.make_async_remote_copy(
            src_ref=blocks.at[q, d],
            dst_ref=moved.at[me, :, pl.ds(q * part_rows, part_rows)],
            send_sem=block_send.at[q, d],
            recv_sem=block_recv.at[q, me],
            device_id={"sector": lax.rem(me + 1 + d, parts)},
            device_id_type=MESH,
        )

    def own_block(q):
        return pltpu.make_async_copy(
            blocks.at[q, parts - 1],
            moved.at[me, :, pl.ds(q * part_rows, part_rows)],
            block_send.at[q, parts - 1],
        )

    def start(copy):
        copy.start()

    for q in range(SHIFTS):
        shift(q).start()
    for piece in range(states):
        outward(me, piece, True, (0, 1, 2), start)
    load_bond = pltpu.make_async_copy(bond_hbm, bond_ref, local_sem.at[0])
    load_bond.start()
    load_site = pltpu.make_async_copy(site_hbm, own_site, local_sem.at[1])
    load_site.start()
    load_site.wait()
    keep_site = pltpu.make_async_copy(own_site, gathered.at[me], local_sem.at[1])
    keep_site.start()
    load_bond.wait()

    def product(q):
        shift(q).wait_recv()
        span = pl.ds(q * part_rows, part_rows)
        x = right[:, span].reshape(width * part_rows, bond)

        def step(d, carry):
            j = lax.rem(me + 1 + d, parts)
            out = lax.dot_general(
                x,
                bond_ref[pl.ds(pl.multiple_of(j * columns, columns), columns), :],
                (((1,), (1,)), ((), ())),
                preferred_element_type=jnp.float32,
            )
            blocks[q, d] = out.astype(jnp.bfloat16).reshape(width, part_rows, columns)

            @pl.when(d > 0)
            def _():
                block(q, d - 1).start()

            return carry

        lax.fori_loop(0, parts, step, 0)
        own_block(q).start()

    def relay(distance, piece):
        for way, source in ((0, me - 2 * distance), (1, me + 2 * distance)):
            there = z >= distance if way == 0 else z + distance < line

            @pl.when(there)
            def _():
                hop(way, source, piece, twin).wait_recv()
                outward(source, piece, False, (way, 2), start)

    ticks = [(distance, piece) for distance in range(1, line) for piece in range(states)]
    for i, (distance, piece) in enumerate(ticks):
        relay(distance, piece)
        if i < SHIFTS:
            product(i)
    for q in range(len(ticks), SHIFTS):
        product(q)
    for other in range(line):
        for piece in range(states):
            hop(2, 2 * other + 1 - y, piece, twin).wait_recv()
    keep_site.wait()

    tile = min(rows, LANES)
    pltpu.emit_pipeline(
        functools.partial(carried_body, mix_ref),
        grid=(rows // tile, parts),
        in_specs=[
            pl.BlockSpec((width, tile, bond), lambda i, j: (0, i, 0)),
            pl.BlockSpec((parts, states, depth, columns), lambda i, j: (0, 0, 0, j)),
        ],
        out_specs=[
            pl.BlockSpec((1, width // CHUNKS, states, tile, columns), lambda i, j: (j, 0, 0, i, 0))
        ] * CHUNKS,
    )(left_hbm, gathered, *carried)

    for q in range(SHIFTS):
        shift(q).wait_send()
    for piece in range(states):
        outward(me, piece, True, (0, 1, 2), lambda copy: copy.wait_send())
    for distance, piece in ticks:
        for way, source in ((0, me - 2 * distance), (1, me + 2 * distance)):
            there = z >= distance if way == 0 else z + distance < line

            @pl.when(there)
            def _():
                outward(source, piece, False, (way, 2), lambda copy: copy.wait_send())
    for q in range(SHIFTS):
        own_block(q).wait()

        def finish(d, carry):
            block(q, d).wait_send()
            source = lax.rem(me + 1 + d, parts)
            pltpu.make_async_remote_copy(
                src_ref=blocks.at[q, d],
                dst_ref=moved.at[source, :, pl.ds(q * part_rows, part_rows)],
                send_sem=block_send.at[q, d],
                recv_sem=block_recv.at[q, source],
                device_id={"sector": source},
                device_id_type=MESH,
            ).wait_recv()
            return carry

        lax.fori_loop(0, parts - 1, finish, 0)


def head(env_left, site, mpo, env_right, bond_tensor, parts):
    width, rows, bond = env_left.shape
    states, depth, _ = site.shape
    columns = bond // parts
    eye = jnp.eye(GROUP, dtype=jnp.float32)
    side = width * states * GROUP
    mix = jnp.einsum("vwst,ij->wsitvj", mpo, eye, precision=lax.Precision.HIGHEST).reshape(side, side)
    part_rows = rows // SHIFTS
    carried = jax.ShapeDtypeStruct((parts, width // CHUNKS, states, rows, columns), jnp.bfloat16)
    anywhere = pl.BlockSpec(memory_space=pl.ANY)
    dma = pltpu.SemaphoreType.DMA
    return pl.pallas_call(
        head_kernel,
        in_specs=[pl.BlockSpec(memory_space=pltpu.VMEM)] + [anywhere] * 4,
        out_specs=[anywhere] * (2 + CHUNKS),
        out_shape=[
            jax.ShapeDtypeStruct((parts, states, depth, bond), jnp.bfloat16),
            jax.ShapeDtypeStruct((parts, width, rows, columns), jnp.bfloat16),
        ] + [carried] * CHUNKS,
        scratch_shapes=[
            pltpu.VMEM((width, rows, bond), jnp.bfloat16),
            pltpu.VMEM((bond, bond), jnp.bfloat16),
            pltpu.VMEM((SHIFTS, parts, width, part_rows, columns), jnp.bfloat16),
            pltpu.VMEM((states, depth, bond), jnp.bfloat16),
            dma((SHIFTS,)),
            dma((SHIFTS,)),
            dma((3, parts, states)),
            dma((parts, states)),
            dma((SHIFTS, parts)),
            dma((SHIFTS, parts)),
            dma((2,)),
        ],
        compiler_params=pltpu.CompilerParams(
            vmem_limit_bytes=VMEM_LIMIT, collective_id=0, has_side_effects=True
        ),
        cost_estimate=pl.CostEstimate(
            flops=3 * width * rows * bond * bond * states,
            bytes_accessed=128 * 1024 * 1024,
            transcendentals=0,
        ),
    )(mix, env_right, site, bond_tensor, env_left)


def env_kernel(x_ref, site_ref, *rest):
    out_ref, turned = rest[-2:]
    parts, count, states, depth, columns = x_ref.shape

    @pl.when(pl.program_id(0) == 0)
    def _():
        for n in range(parts):
            for s in range(states):
                at = (n * states + s) * depth
                for v in range(count):
                    turned[v * columns : (v + 1) * columns, at : at + depth] = x_ref[n, v, s].T

    site = site_ref[...].reshape(parts * states * depth, site_ref.shape[-1])
    total = jnp.dot(turned[...], site, preferred_element_type=jnp.float32)
    out_ref[...] = total.astype(jnp.bfloat16).reshape(out_ref.shape)


def env_chunk(moved, gathered, previous, chunk, width, tile):
    parts, count, states, depth, columns = moved.shape
    bond = gathered.shape[-1]
    operands = (moved, gathered) + (() if previous is None else (previous,))
    specs = [
        pl.BlockSpec(moved.shape, lambda j: (0, 0, 0, 0, 0), pipeline_mode=pl.Buffered(1)),
        pl.BlockSpec((parts, states, depth, tile), lambda j: (0, 0, 0, j)),
    ]
    if previous is not None:
        specs.append(pl.BlockSpec(memory_space=pl.ANY))
    return pl.pallas_call(
        env_kernel,
        grid=(bond // tile,),
        in_specs=specs,
        out_specs=pl.BlockSpec((count, columns, tile), lambda j: (chunk, 0, j)),
        out_shape=jax.ShapeDtypeStruct((width, columns, bond), jnp.bfloat16),
        scratch_shapes=[pltpu.VMEM((count * columns, parts * states * depth), jnp.bfloat16)],
        input_output_aliases={} if previous is None else {2: 0},
        compiler_params=pltpu.CompilerParams(vmem_limit_bytes=VMEM_LIMIT),
        cost_estimate=pl.CostEstimate(
            flops=2 * count * columns * parts * states * depth * bond,
            bytes_accessed=32 * 1024 * 1024,
            transcendentals=0,
        ),
    )(*operands)


def local(env_left, site_tensor, mpo_tensor, env_right, bond_tensor):
    parts = lax.axis_size("sector")
    width, rows, bond = env_left.shape[1:]
    columns = bond // parts
    half = rows // CHUNKS
    gathered, bond_moved, *carried = head(
        env_left[0], site_tensor[0].transpose(1, 0, 2), mpo_tensor[0],
        env_right[0], bond_tensor[0], parts,
    )
    moved = []
    for i in range(CHUNKS):
        moved.append(swap(carried[i]))
    env_new = None
    for i in range(CHUNKS):
        env_new = env_chunk(moved[i], gathered, env_new, i, width, 2 * LANES)
    image_rows = []
    for i in range(CHUNKS):
        image = jnp.einsum(
            "wkda,nwbk->dnba",
            env_new.reshape(width, columns, parts, columns),
            bond_moved[:, :, i * half : (i + 1) * half],
            preferred_element_type=jnp.float32,
        ).astype(jnp.bfloat16).reshape(parts, parts * half, columns)
        image_rows.append(lax.psum_scatter(image, "sector", scatter_dimension=0, tiled=False))
    image_rows = jnp.stack(
        [x.reshape(parts, half, columns) for x in image_rows], axis=1
    ).reshape(bond, columns).T
    return (env_new[None], image_rows[None])


def plain_local(env_left, site_tensor, mpo_tensor, env_right, bond_tensor):
    width = env_left.shape[1]
    states = site_tensor.shape[2]
    gathered = lax.all_gather(site_tensor, "sector", axis=1, tiled=True)[0]
    half_done = jnp.einsum(
        "wak,ksc->wasc", env_left[0], gathered, preferred_element_type=jnp.float32
    )
    carried = jnp.einsum(
        "vwst,vatc->wsac", mpo_tensor[0], half_done, precision=lax.Precision.HIGHEST
    ).astype(jnp.bfloat16)
    carried = carried.reshape((width * states,) + carried.shape[2:])
    right_next = shifted(env_right, "region", -1)[0]
    bond_right = jnp.einsum(
        "wbc,kc->wbk", right_next, bond_tensor[0], preferred_element_type=jnp.float32
    ).astype(jnp.bfloat16)
    carried_moved = lax.all_to_all(carried, "sector", split_axis=2, concat_axis=1, tiled=True)
    bond_moved = lax.all_to_all(bond_right, "sector", split_axis=2, concat_axis=1, tiled=True)
    carried_moved = carried_moved.reshape((width, states) + carried_moved.shape[1:])
    env_new = jnp.einsum(
        "wsac,asb->wcb", carried_moved, gathered, preferred_element_type=jnp.float32
    ).astype(jnp.bfloat16)
    image_rows = lax.psum_scatter(
        jnp.einsum("wka,wbk->ab", env_new, bond_moved, preferred_element_type=jnp.float32),
        "sector",
        scatter_dimension=0,
        tiled=True,
    )
    return (env_new[None], image_rows.astype(jnp.bfloat16)[None])


def solution(mesh):
    def body(env_left, site_tensor, mpo_tensor, env_right, bond_tensor):
        width, rows, bond = env_left.shape[1:]
        columns = bond // mesh.shape["sector"]
        tiled = rows % LANES == 0 and columns % LANES == 0 and width % CHUNKS == 0 and rows % (16 * SHIFTS) == 0
        tiled = tiled and mesh.shape["sector"] % 2 == 0 and mesh.shape["region"] > 2
        step = local if tiled else plain_local
        return step(env_left, site_tensor, mpo_tensor, env_right, bond_tensor)

    return jax.shard_map(
        body,
        mesh=mesh,
        in_specs=(
            P("region", None, "sector", None),
            P("region", "sector", None, None),
            P("region", None, None, None, None),
            P("region", None, "sector", None),
            P("region", None, None),
        ),
        out_specs=(P("region", None, "sector", None), P("region", "sector", None)),
        check_vma=False,
    )
```

profile of v0, /device:TPU:0, one launch (start us, length us, event | category | flops | bytes accessed | tf_op | source)
XLA Modules:
  0.0 968.5 jit_solution(8927677616238022190)
XLA Ops:
  7.2 0.8 copy.18
  8.0 0.2 multiply_bitcast_fusion
  8.2 1.5 reshape.20.mix_ref
  9.7 3.8 copy.44
  13.5 349.0 %shard_map.68 = (bf16[8,2,256,2048]{3,2,1,0:T(8,128)(2,1)}, bf16[8,8,256,256]{3,2,1,0:T(8,128)(2,1)}, bf16[8,4,2,256,256]{4,3,2,1,0:T(8,128)(2,1)}, bf16[8,4,2,256,256]{4,3,2,1,0:T(8,128)(2,1)}) custom-call(f32[256,256]{1,0:T(8,128)} %reshape.20.mix_ref, bf16[8,256,2048]{2,1,0:T(8,128)(2,1)} %bitcast.76, bf16[2,256,2048]{2,1,0:T(8,128)(2,1)} %bitcast.72, ...), custom_call_target="tpu_custom_call" | custom-call | flops 51539607552 | bytes 134217728 | tf_op jit(solution)/shard_map/pallas_call | solution.py:252
  362.5 189.2 %all_to_all.10.x_ref = bf16[8,4,2,256,256]{4,3,2,1,0:T(8,128)(2,1)} all-to-all(bf16[8,4,2,256,256]{4,3,2,1,0:T(8,128)(2,1)} %get-tuple-element.8), channel_id=1, replica_groups=mesh['region'=4,'sector'=8] {'sector'}, dimensions={0} | all-to-all | bytes 16777216 | tf_op jit(solution)/shard_map/all_to_all | solution.py:25
  551.7 4.9 all-to-all-start
  556.6 0.2 reduce-scatter.5.cloned.1.call-start
  556.9 26.0 %shard_map.69.rest_0_ = bf16[8,256,2048]{2,1,0:T(8,128)(2,1)} custom-call(bf16[8,4,2,256,256]{4,3,2,1,0:T(8,128)(2,1)} %all_to_all.10.x_ref, bf16[8,2,256,2048]{3,2,1,0:T(8,128)(2,1)} %get-tuple-element.7.site_ref), custom_call_target="tpu_custom_call" | custom-call | flops 17179869184 | bytes 33554432 | tf_op jit(solution)/shard_map/pallas_call | solution.py:311
  582.9 156.4 %all-to-all-done.x_ref = bf16[8,4,2,256,256]{4,3,2,1,0:T(8,128)(2,1)} async-done(((bf16[8,4,2,256,256]{4,3,2,1,0:T(8,128)(2,1)}), bf16[8,4,2,256,256]{4,3,2,1,0:T(8,128)(2,1)}, u32[]{:S(2)}, u32[]{:S(2)}) %all-to-all-start) | async-done | bytes 8388640 | tf_op jit(solution)/shard_map/all_to_all | solution.py:25
  739.3 26.0 %shard_map.70 = bf16[8,256,2048]{2,1,0:T(8,128)(2,1)} custom-call(bf16[8,4,2,256,256]{4,3,2,1,0:T(8,128)(2,1)} %all-to-all-done.x_ref, bf16[8,2,256,2048]{3,2,1,0:T(8,128)(2,1)} %get-tuple-element.7.site_ref, bf16[8,256,2048]{2,1,0:T(8,128)(2,1)} %shard_map.69.rest_0_), custom_call_target="tpu_custom_call", output_to_operand_aliasing={{}: (2, {})} | custom-call | flops 17179869184 | bytes 33554432 | tf_op jit(solution)/shard_map/pallas_call | solution.py:311
  765.3 12.5 %fusion.5 = bf16[8,8,128,256]{3,2,0,1:T(8,128)(2,1)S(1)} fusion(bf16[8,32,8,8,256]{4,3,2,1,0:T(8,128)(2,1)} %bitcast.79, bf16[8,8,256,256]{3,2,1,0:T(8,128)(2,1)} %get-tuple-element.9), kind=kOutput, calls=%fused_computation.8 | convolution fusion | flops 8592031744 | bytes 16777216 | tf_op jit(solution)/shard_map/wkda,nwbk->dnba/dot_general | solution.py:345
  777.8 2.4 copy.23
  780.2 0.0 reduce-scatter.5.cloned.1.call-update
  780.3 0.3 reduce-scatter.3.cloned.1.call-start
  780.5 12.5 %fusion.4 = bf16[8,8,128,256]{3,2,0,1:T(8,128)(2,1)S(1)} fusion(bf16[8,32,8,8,256]{4,3,2,1,0:T(8,128)(2,1)} %bitcast.80, bf16[8,8,256,256]{3,2,1,0:T(8,128)(2,1)} %get-tuple-element.9), kind=kOutput, calls=%fused_computation.7 | convolution fusion | flops 8592031744 | bytes 16777216 | tf_op jit(solution)/shard_map/wkda,nwbk->dnba/dot_general | solution.py:345
  793.1 2.5 copy.21
  795.5 0.0 reduce-scatter.3.cloned.1.call-update
  795.6 71.6 %reduce-scatter.5.cloned.1.call-done = bf16[1,1024,256]{2,1,0:T(8,128)(2,1)} async-done(((bf16[8,1024,256]{2,1,0:T(8,128)(2,1)}), bf16[1,1024,256]{2,1,0:T(8,128)(2,1)}) %reduce-scatter.5.cloned.1.call-update) | async-done | bytes 524304 | tf_op jit(solution)/shard_map/reduce_scatter | solution.py:351
  867.2 91.6 %reduce-scatter.3.cloned.1.call-done = bf16[1,1024,256]{2,1,0:T(8,128)(2,1)} async-done(((bf16[8,1024,256]{2,1,0:T(8,128)(2,1)}), bf16[1,1024,256]{2,1,0:T(8,128)(2,1)}) %reduce-scatter.3.cloned.1.call-update) | async-done | bytes 524304 | tf_op jit(solution)/shard_map/reduce_scatter | solution.py:351
  958.8 1.3 pad_maximum_fusion
  960.1 0.1 copy.24
  960.2 1.4 copy.25
  (1 shorter events, 0.0 us)
Async XLA Ops:
  551.7 187.6 %all-to-all-start = ((bf16[8,4,2,256,256]{4,3,2,1,0:T(8,128)(2,1)}), bf16[8,4,2,256,256]{4,3,2,1,0:T(8,128)(2,1)}, u32[]{:S(2)}, u32[]{:S(2)}) async-start(bf16[8,4,2,256,256]{4,3,2,1,0:T(8,128)(2,1)} %get-tuple-element.6), calls=%async_computation | async-start | bytes 16777216 | tf_op jit(solution)/shard_map/all_to_all | solution.py:25
  556.6 310.6 %reduce-scatter.5.cloned.1.call-start = ((), (), s32[]{:S(2)}) async-start(), calls=%async_computation.5 | async-start | bytes 4718592 | tf_op jit(solution)/shard_map/reduce_scatter | solution.py:351
  780.3 178.5 %reduce-scatter.3.cloned.1.call-start = ((), (), s32[]{:S(2)}) async-start(), calls=%async_computation.4 | async-start | bytes 4718592 | tf_op jit(solution)/shard_map/reduce_scatter | solution.py:351
Sparse Core Ops, SparseCore 0:
  780.4 86.7 reduce-scatter.4
  870.8 87.9 reduce-scatter.2
where the time goes:
time: 969 us; the launch traced here: 968 us
  Pallas kernels  401 us (41%)
  waiting for transfers between devices  320 us (33%)
  blocking collectives  189 us (20%)
  matrix products  25 us (3%)
  between operations  14.1 us (1%)
  local copies, waits for them, and re-layouts  12.5 us (1%)
    pallas_call x1, Pallas kernels, head(): pl.pallas_call(head_kernel, in_specs=[pl.BlockSpec(memory_space=pltpu.VME...  349 us
    all_to_all x1, blocking collectives, swap(): lax.all_to_all(blocks, 'sector', split_axis=0, concat_axis=0, tiled=True)  189 us
    reduce_scatter x2, waiting for transfers between devices, local(): lax.psum_scatter(image, 'sector', scatter_dimension=0, tiled=False)  163 us
    all_to_all x1, waiting for transfers between devices, swap(): lax.all_to_all(blocks, 'sector', split_axis=0, concat_axis=0, tiled=True)  156 us
    pallas_call x2, Pallas kernels, env_chunk(): pl.pallas_call(env_kernel, grid=(bond // tile,), in_specs=specs, out_spec...  52 us
    dot_general x2, matrix products, local(): jnp.einsum('wkda,nwbk->dnba', env_new.reshape(width, columns, parts, colu...  25 us
  transfers between devices with their start and end apart: 3, of which 3 were waited for; matrix products, arithmetic and copies ran while one was open for 2% of the time, Pallas kernels for 3%

commit v1 on v0

--- a/solution.py
+++ b/solution.py
@@ -7,11 +7,13 @@
 from jax.experimental.pallas import tpu as pltpu
 from jax.sharding import PartitionSpec as P
 
-
 GROUP = 16
 LANES = 128
-CHUNKS = 2
+CHUNKS = 4
 SHIFTS = 4
+EARLY = 2
+HOLD = (0, 5)
+AHEAD = 2
 VMEM_LIMIT = 60 * 1024 * 1024
 
 
@@ -19,10 +21,6 @@
     devices = range(lax.axis_size(axis))
     route = [((i - distance) % len(devices), i) for i in devices]
     return lax.ppermute(block, axis, route)
-
-
-def swap(blocks):
-    return lax.all_to_all(blocks, "sector", split_axis=0, concat_axis=0, tiled=True)
 
 
 MESH = pl.DeviceIdType.MESH
@@ -57,7 +55,7 @@
 
 def head_kernel(
     mix_ref, right_hbm, site_hbm, bond_hbm, left_hbm,
-    gathered, moved, *rest,
+    gathered, moved, late, *rest,
 ):
     carried = rest[:CHUNKS]
     (right, bond_ref, blocks, own_site, shift_send, shift_recv, site_send, site_recv,
@@ -120,18 +118,19 @@
     def block(q, d):
         return pltpu.make_async_remote_copy(
             src_ref=blocks.at[q, d],
-            dst_ref=moved.at[me, :, pl.ds(q * part_rows, part_rows)],
+            dst_ref=moved.at[q, me],
             send_sem=block_send.at[q, d],
             recv_sem=block_recv.at[q, me],
             device_id={"sector": lax.rem(me + 1 + d, parts)},
             device_id_type=MESH,
         )
 
-    def own_block(q):
+    def stored(q, d):
+        j = lax.rem(me + 1 + d, parts)
         return pltpu.make_async_copy(
-            blocks.at[q, parts - 1],
-            moved.at[me, :, pl.ds(q * part_rows, part_rows)],
-            block_send.at[q, parts - 1],
+            blocks.at[q, d],
+            moved.at[q, j] if q < EARLY else late.at[q - EARLY, j],
+            block_send.at[q, d],
         )
 
     def start(copy):
@@ -164,15 +163,18 @@
                 preferred_element_type=jnp.float32,
             )
             blocks[q, d] = out.astype(jnp.bfloat16).reshape(width, part_rows, columns)
-
-            @pl.when(d > 0)
-            def _():
-                block(q, d - 1).start()
-
             return carry
 
         lax.fori_loop(0, parts, step, 0)
-        own_block(q).start()
+
+    def dispatch(q):
+        if q < EARLY:
+            for d in range(parts - 1):
+                block(q, d).start()
+            stored(q, parts - 1).start()
+        else:
+            for d in range(parts):
+                stored(q, d).start()
 
     def relay(distance, piece):
         for way, source in ((0, me - 2 * distance), (1, me + 2 * distance)):
@@ -188,8 +190,11 @@
         relay(distance, piece)
         if i < SHIFTS:
             product(i)
-    for q in range(len(ticks), SHIFTS):
-        product(q)
+            if i >= EARLY:
+                dispatch(i)
+        for q in range(EARLY):
+            if HOLD[q] == i:
+                dispatch(q)
     for other in range(line):
         for piece in range(states):
             hop(2, 2 * other + 1 - y, piece, twin).wait_recv()
@@ -219,15 +224,18 @@
             @pl.when(there)
             def _():
                 outward(source, piece, False, (way, 2), lambda copy: copy.wait_send())
-    for q in range(SHIFTS):
-        own_block(q).wait()
+    for q in range(EARLY, SHIFTS):
+        for d in range(parts):
+            stored(q, d).wait()
+    for q in range(EARLY):
+        stored(q, parts - 1).wait()
 
         def finish(d, carry):
             block(q, d).wait_send()
             source = lax.rem(me + 1 + d, parts)
             pltpu.make_async_remote_copy(
                 src_ref=blocks.at[q, d],
-                dst_ref=moved.at[source, :, pl.ds(q * part_rows, part_rows)],
+                dst_ref=moved.at[q, source],
                 send_sem=block_send.at[q, d],
                 recv_sem=block_recv.at[q, source],
                 device_id={"sector": source},
@@ -252,10 +260,11 @@
     return pl.pallas_call(
         head_kernel,
         in_specs=[pl.BlockSpec(memory_space=pltpu.VMEM)] + [anywhere] * 4,
-        out_specs=[anywhere] * (2 + CHUNKS),
+        out_specs=[anywhere] * (3 + CHUNKS),
         out_shape=[
             jax.ShapeDtypeStruct((parts, states, depth, bond), jnp.bfloat16),
-            jax.ShapeDtypeStruct((parts, width, rows, columns), jnp.bfloat16),
+            jax.ShapeDtypeStruct((EARLY, parts, width, part_rows, columns), jnp.bfloat16),
+            jax.ShapeDtypeStruct((SHIFTS - EARLY, parts, width, part_rows, columns), jnp.bfloat16),
         ] + [carried] * CHUNKS,
         scratch_shapes=[
             pltpu.VMEM((width, rows, bond), jnp.bfloat16),
@@ -281,77 +290,306 @@
     )(mix, env_right, site, bond_tensor, env_left)
 
 
-def env_kernel(x_ref, site_ref, *rest):
-    out_ref, turned = rest[-2:]
-    parts, count, states, depth, columns = x_ref.shape
-
-    @pl.when(pl.program_id(0) == 0)
-    def _():
-        for n in range(parts):
-            for s in range(states):
-                at = (n * states + s) * depth
-                for v in range(count):
-                    turned[v * columns : (v + 1) * columns, at : at + depth] = x_ref[n, v, s].T
-
-    site = site_ref[...].reshape(parts * states * depth, site_ref.shape[-1])
-    total = jnp.dot(turned[...], site, preferred_element_type=jnp.float32)
-    out_ref[...] = total.astype(jnp.bfloat16).reshape(out_ref.shape)
-
-
-def env_chunk(moved, gathered, previous, chunk, width, tile):
-    parts, count, states, depth, columns = moved.shape
-    bond = gathered.shape[-1]
-    operands = (moved, gathered) + (() if previous is None else (previous,))
-    specs = [
-        pl.BlockSpec(moved.shape, lambda j: (0, 0, 0, 0, 0), pipeline_mode=pl.Buffered(1)),
-        pl.BlockSpec((parts, states, depth, tile), lambda j: (0, 0, 0, j)),
-    ]
-    if previous is not None:
-        specs.append(pl.BlockSpec(memory_space=pl.ANY))
+def rest_kernel(gathered, moved, late, *refs):
+    carried = refs[:CHUNKS]
+    env_out, image_out, late_moved = refs[CHUNKS : CHUNKS + 3]
+    landed = refs[CHUNKS + 3 : 2 * CHUNKS + 3]
+    (x, turned, env, bond_in, keep, pair_out, pair_in, line_out, line_in, done,
+     swap_send, swap_recv, late_send, late_recv, pair_send, pair_recv, line_send, line_recv,
+     load_sem, env_sem, out_sem) = refs[2 * CHUNKS + 3 :]
+    parts, states, depth, bond = gathered.shape
+    _, count, _, _, columns = landed[0].shape
+    width = count * CHUNKS
+    part_rows = moved.shape[3]
+    line = parts // 2
+    group = line
+    steps = SHIFTS * 2
+    me = lax.axis_index("sector")
+    z, y = me // 2, lax.rem(me, 2)
+    twin = 2 * z + 1 - y
+
+    barrier = pltpu.get_barrier_semaphore()
+    for d in range(1, parts):
+        pl.semaphore_signal(
+            barrier, inc=1, device_id={"sector": lax.rem(me + d, parts)}, device_id_type=MESH
+        )
+    pl.semaphore_wait(barrier, parts - 1)
+
+    def remote(src, dst, send, recv, target):
+        return pltpu.make_async_remote_copy(
+            src_ref=src, dst_ref=dst, send_sem=send, recv_sem=recv,
+            device_id={"sector": target}, device_id_type=MESH,
+        )
+
+    def batch_copy(b, d, receiving=False):
+        j = lax.rem(me + 1 + d, parts)
+        owner = j if receiving else me
+        if b < CHUNKS:
+            return remote(
+                carried[b].at[j], landed[b].at[owner],
+                swap_send.at[b, d], swap_recv.at[b, owner], j,
+            )
+        q = b - CHUNKS
+        return remote(
+            late.at[q, j], late_moved.at[q, owner],
+            late_send.at[q, d], late_recv.at[q, owner], j,
+        )
+
+    batches = CHUNKS + SHIFTS - EARLY
+
+    def dispatch(b):
+        if b < batches:
+            for d in range(parts - 1):
+                batch_copy(b, d).start()
+
+    def collect(b):
+        for d in range(parts - 1):
+            batch_copy(b, d, True).wait_recv()
+        dispatch(b + AHEAD)
+
+    for b in range(AHEAD):
+        dispatch(b)
+
+    def fill(b):
+        own = pltpu.make_async_copy(carried[b].at[me], x.at[me], load_sem.at[parts - 1])
+        own.start()
+        copies = [own]
+        for d in range(parts - 1):
+            n = lax.rem(me + 1 + d, parts)
+            copies.append(pltpu.make_async_copy(landed[b].at[n], x.at[n], load_sem.at[d]))
+            copies[-1].start()
+        for copy in copies:
+            copy.wait()
+
+    def turn(n, carry):
+        for s in range(states):
+            at = pl.multiple_of((n * states + s) * depth, depth)
+            for v in range(count):
+                turned[v * columns : (v + 1) * columns, pl.ds(at, depth)] = x[n, v, s].T
+        return carry
+
+    def env_body(site_ref, out_ref):
+        site = site_ref[...].reshape(parts * states * depth, site_ref.shape[-1])
+        total = jnp.dot(turned[...], site, preferred_element_type=jnp.float32)
+        out_ref[...] = total.astype(jnp.bfloat16).reshape(out_ref.shape)
+
+    def reload(b):
+        span = pl.ds(b * count, count)
+        return pltpu.make_async_copy(env_out.at[span], env.at[span], env_sem.at[b])
+
+    tile = 2 * LANES
+    for b in range(CHUNKS):
+        collect(b)
+        fill(b)
+        lax.fori_loop(0, parts, turn, 0)
+        pltpu.emit_pipeline(
+            env_body,
+            grid=(bond // tile,),
+            in_specs=[pl.BlockSpec((parts, states, depth, tile), lambda j: (0, 0, 0, j))],
+            out_specs=[pl.BlockSpec((count, columns, tile), lambda j: (0, 0, j))],
+        )(gathered, env_out.at[pl.ds(b * count, count)])
+        reload(b).start()
+    for b in range(CHUNKS):
+        reload(b).wait()
+
+    def pair_copy(u):
+        return remote(pair_out.at[u], pair_in.at[u], pair_send.at[u], pair_recv.at[u], twin)
+
+    def line_copy(u, t, way):
+        slot = t + 1 if way == 0 else t
+        return remote(
+            line_out.at[u, t], line_in.at[u, slot], line_send.at[u, t], line_recv.at[u, slot],
+            me + 2 if way == 0 else me - 2,
+        )
+
+    def dot(a, b):
+        return jnp.dot(a, b, preferred_element_type=jnp.float32)
+
+    def image(u):
+        q, part = u // 2, u % 2
+        for i in range(group):
+            n = part * group + i
+            if q < EARLY:
+                pltpu.make_async_copy(moved.at[q, n], bond_in.at[i], load_sem.at[i]).start()
+            else:
+                mine = n == me
+
+                @pl.when(mine)
+                def _():
+                    pltpu.make_async_copy(
+                        late.at[q - EARLY, n], bond_in.at[i], load_sem.at[i]
+                    ).start()
+
+                @pl.when(jnp.logical_not(mine))
+                def _():
+                    pltpu.make_async_copy(
+                        late_moved.at[q - EARLY, n], bond_in.at[i], load_sem.at[i]
+                    ).start()
+
+        for i in range(group):
+            pltpu.make_async_copy(moved.at[0, 0], bond_in.at[i], load_sem.at[i]).wait()
+        left = jnp.concatenate(
+            [bond_in[:, w].reshape(group * part_rows, columns) for w in range(width)], axis=1
+        )
+        for t in range(line):
+            at = pl.multiple_of((2 * t + 1 - y) * columns, columns)
+            pair_out[u, t] = dot(
+                left, env[:, :, pl.ds(at, columns)].reshape(width * columns, columns)
+            ).astype(jnp.bfloat16)
+        for t in range(line):
+            at = pl.multiple_of((2 * t + y) * columns, columns)
+            keep[u, t] = dot(left, env[:, :, pl.ds(at, columns)].reshape(width * columns, columns))
+        pair_copy(u).start()
+
+    def paired(u):
+        pair_copy(u).wait_recv()
+        keep[u] = keep[u] + pair_in[u].astype(jnp.float32)
+
+    def relay(s, way):
+        first = z if way == 0 else line - 1 - z
+        u = s - 1 - first
+        live = jnp.logical_and(u >= 0, u < steps)
+        for t in range(line):
+            sends = jnp.logical_and(live, t > z if way == 0 else t < z)
+
+            @pl.when(jnp.logical_and(sends, first == 0))
+            def _():
+                line_out[u, t] = keep[u, t].astype(jnp.bfloat16)
+
+            @pl.when(jnp.logical_and(sends, first > 0))
+            def _():
+                slot = t + 1 if way == 0 else t
+                line_copy(u, t, way).wait_recv()
+                line_out[u, t] = (
+                    keep[u, t] + line_in[u, slot].astype(jnp.float32)
+                ).astype(jnp.bfloat16)
+
+    def send_on(s, way):
+        first = z if way == 0 else line - 1 - z
+        u = s - 1 - first
+        live = jnp.logical_and(u >= 0, u < steps)
+        for t in range(line):
+
+            @pl.when(jnp.logical_and(live, t > z if way == 0 else t < z))
+            def _():
+                line_copy(u, t, way).start()
+
+    def result(u):
+        return pltpu.make_async_copy(done.at[u], image_out.at[u], out_sem.at[u])
+
+    def total(u):
+        @pl.when(z > 0)
+        def _():
+            line_copy(u, z, 0).wait_recv()
+            keep[u, z] = keep[u, z] + line_in[u, z + 1].astype(jnp.float32)
+
+        @pl.when(z < line - 1)
+        def _():
+            line_copy(u, z, 1).wait_recv()
+            keep[u, z] = keep[u, z] + line_in[u, z].astype(jnp.float32)
+
+        done[u] = keep[u, z].astype(jnp.bfloat16)
+
+    for s in range(steps + line):
+        if s < steps:
+            if s % 2 == 0 and s // 2 >= EARLY:
+                collect(CHUNKS + s // 2 - EARLY)
+            image(s)
+        if 1 <= s <= steps:
+            paired(s - 1)
+        relay(s, 0)
+        relay(s, 1)
+        if s >= line:
+            total(s - line)
+        send_on(s, 0)
+        send_on(s, 1)
+        if s >= line:
+            result(s - line).start()
+
+    for b in range(batches):
+        for d in range(parts - 1):
+            batch_copy(b, d).wait_send()
+    for u in range(steps):
+        pair_copy(u).wait_send()
+        result(u).wait()
+        for t in range(line):
+            @pl.when(t > z)
+            def _():
+                line_copy(u, t, 0).wait_send()
+
+            @pl.when(t < z)
+            def _():
+                line_copy(u, t, 1).wait_send()
+
+
+def rest_of(gathered, moved, late, carried):
+    parts, states, depth, bond = gathered.shape
+    _, count, _, _, columns = carried[0].shape
+    width = count * CHUNKS
+    part_rows = moved.shape[3]
+    line = parts // 2
+    steps = SHIFTS * 2
+    block = (line * part_rows, columns)
+    anywhere = pl.BlockSpec(memory_space=pl.ANY)
+    dma = pltpu.SemaphoreType.DMA
+    bf16 = jnp.bfloat16
     return pl.pallas_call(
-        env_kernel,
-        grid=(bond // tile,),
-        in_specs=specs,
-        out_specs=pl.BlockSpec((count, columns, tile), lambda j: (chunk, 0, j)),
-        out_shape=jax.ShapeDtypeStruct((width, columns, bond), jnp.bfloat16),
-        scratch_shapes=[pltpu.VMEM((count * columns, parts * states * depth), jnp.bfloat16)],
-        input_output_aliases={} if previous is None else {2: 0},
-        compiler_params=pltpu.CompilerParams(vmem_limit_bytes=VMEM_LIMIT),
+        rest_kernel,
+        in_specs=[anywhere] * (3 + CHUNKS),
+        out_specs=[anywhere] * (3 + CHUNKS),
+        out_shape=[
+            jax.ShapeDtypeStruct((width, columns, bond), bf16),
+            jax.ShapeDtypeStruct((steps,) + block, bf16),
+            jax.ShapeDtypeStruct(late.shape, bf16),
+        ] + [jax.ShapeDtypeStruct(c.shape, bf16) for c in carried],
+        scratch_shapes=[
+            pltpu.VMEM(carried[0].shape, bf16),
+            pltpu.VMEM((count * columns, parts * states * depth), bf16),
+            pltpu.VMEM((width, columns, bond), bf16),
+            pltpu.VMEM((line, width, part_rows, columns), bf16),
+            pltpu.VMEM((steps, line) + block, jnp.float32),
+            pltpu.VMEM((steps, line) + block, bf16),
+            pltpu.VMEM((steps, line) + block, bf16),
+            pltpu.VMEM((steps, line) + block, bf16),
+            pltpu.VMEM((steps, line + 1) + block, bf16),
+            pltpu.VMEM((steps,) + block, bf16),
+            dma((CHUNKS, parts)),
+            dma((CHUNKS, parts)),
+            dma((SHIFTS - EARLY, parts)),
+            dma((SHIFTS - EARLY, parts)),
+            dma((steps,)),
+            dma((steps,)),
+            dma((steps, line)),
+            dma((steps, line + 1)),
+            dma((parts,)),
+            dma((CHUNKS,)),
+            dma((steps,)),
+        ],
+        compiler_params=pltpu.CompilerParams(
+            vmem_limit_bytes=VMEM_LIMIT, collective_id=1, has_side_effects=True
+        ),
         cost_estimate=pl.CostEstimate(
-            flops=2 * count * columns * parts * states * depth * bond,
-            bytes_accessed=32 * 1024 * 1024,
+            flops=3 * width * columns * parts * states * depth * bond,
+            bytes_accessed=128 * 1024 * 1024,
             transcendentals=0,
         ),
-    )(*operands)
+    )(gathered, moved, late, *carried)
 
 
 def local(env_left, site_tensor, mpo_tensor, env_right, bond_tensor):
     parts = lax.axis_size("sector")
-    width, rows, bond = env_left.shape[1:]
+    _, rows, bond = env_left.shape[1:]
     columns = bond // parts
-    half = rows // CHUNKS
-    gathered, bond_moved, *carried = head(
+    gathered, moved, late, *carried = head(
         env_left[0], site_tensor[0].transpose(1, 0, 2), mpo_tensor[0],
         env_right[0], bond_tensor[0], parts,
     )
-    moved = []
-    for i in range(CHUNKS):
-        moved.append(swap(carried[i]))
-    env_new = None
-    for i in range(CHUNKS):
-        env_new = env_chunk(moved[i], gathered, env_new, i, width, 2 * LANES)
-    image_rows = []
-    for i in range(CHUNKS):
-        image = jnp.einsum(
-            "wkda,nwbk->dnba",
-            env_new.reshape(width, columns, parts, columns),
-            bond_moved[:, :, i * half : (i + 1) * half],
-            preferred_element_type=jnp.float32,
-        ).astype(jnp.bfloat16).reshape(parts, parts * half, columns)
-        image_rows.append(lax.psum_scatter(image, "sector", scatter_dimension=0, tiled=False))
-    image_rows = jnp.stack(
-        [x.reshape(parts, half, columns) for x in image_rows], axis=1
-    ).reshape(bond, columns).T
+    env_new, image, *_ = rest_of(gathered, moved, late, carried)
+    image_rows = (
+        image.reshape(SHIFTS, parts, rows // SHIFTS, columns)
+        .transpose(3, 1, 0, 2)
+        .reshape(columns, bond)
+    )
     return (env_new[None], image_rows[None])
 
 

time: 969 us -> 870 us (0.90); the launches traced: 968 us -> 859 us
  Pallas kernels: 401 us -> 840 us
  waiting for transfers between devices: 320 us -> 0 us
  blocking collectives: 189 us -> 0 us
  matrix products: 25 us -> 0 us
  between operations: 14.1 us -> 1.04 us
    pallas_call x2 -> x1, Pallas kernels: 52 us -> 552 us  [rest_of(): pl.pallas_call(rest_kernel, in_specs=[anywhere] * (3 + CHUNKS), out_specs...]
    all_to_all x1 -> x0, blocking collectives: 189 us -> none  [swap(): lax.all_to_all(blocks, 'sector', split_axis=0, concat_axis=0, tiled=True)]
    reduce_scatter x2 -> x0, waiting for transfers between devices: 163 us -> none  [local(): lax.psum_scatter(image, 'sector', scatter_dimension=0, tiled=False)]
    all_to_all x1 -> x0, waiting for transfers between devices: 156 us -> none  [swap(): lax.all_to_all(blocks, 'sector', split_axis=0, concat_axis=0, tiled=True)]
    pallas_call x1, Pallas kernels: 349 us -> 288 us  [head(): pl.pallas_call(head_kernel, in_specs=[pl.BlockSpec(memory_space=pltpu.VME...]
    dot_general x2 -> x0, matrix products: 25 us -> none  [local(): jnp.einsum('wkda,nwbk->dnba', env_new.reshape(width, columns, parts, colu...]
  transfers between devices with their start and end apart: 3 -> 0, of which waited for: 3 -> 0; matrix products, arithmetic and copies ran while one was open for 2% -> 0% of each run, Pallas kernels for 3% -> 0%
where the time goes in v1:
time: 870 us; the launch traced here: 859 us
  Pallas kernels  840 us (97%)
  local copies, waits for them, and re-layouts  17.3 us (2%)
    pallas_call x1, Pallas kernels, rest_of(): pl.pallas_call(rest_kernel, in_specs=[anywhere] * (3 + CHUNKS), out_specs...  552 us
    pallas_call x1, Pallas kernels, head(): pl.pallas_call(head_kernel, in_specs=[pl.BlockSpec(memory_space=pltpu.VME...  288 us

profile of v1, /device:TPU:0, one launch (start us, length us, event | category | flops | bytes accessed | tf_op | source)
XLA Modules:
  0.0 858.6 jit_solution(2752125049641046343)
XLA Ops:
  0.6 0.8 copy.10
  1.4 0.2 multiply_bitcast_fusion
  1.7 1.5 reshape.10.mix_ref
  3.2 3.8 copy.15
  7.0 288.3 %shard_map.68 = (bf16[8,2,256,2048]{3,2,1,0:T(8,128)(2,1)}, bf16[2,8,8,64,256]{4,3,2,1,0:T(8,128)(2,1)}, bf16[2,8,8,64,256]{4,3,2,1,0:T(8,128)(2,1)}, bf16[8,2,2...) custom-call(f32[256,256]{1,0:T(8,128)} %reshape.10.mix_ref, ...), custom_call_target="tpu_custom_call" | custom-call | flops 51539607552 | bytes 134217728 | tf_op jit(solution)/shard_map/pallas_call | solution.py:260
  295.3 551.8 %shard_map.69 = (bf16[8,256,2048]{2,1,0:T(8,128)(2,1)}, bf16[8,256,256]{2,1,0:T(8,128)(2,1)}, bf16[2,8,8,64,256]{4,3,2,1,0:T(8,128)(2,1)}, bf16[8,2,2,256,256]{4...) custom-call(bf16[8,2,256,2048]{3,2,1,0:T(8,128)(2,1)} %get-tuple-ele, ...), custom_call_target="tpu_custom_call" | custom-call | flops 51539607552 | bytes 134217728 | tf_op jit(solution)/shard_map/pallas_call | solution.py:536
  847.1 1.3 copy.12
  848.4 1.4 copy.13
  849.8 8.4 copy.17
  (1 shorter events, 0.0 us)

commit v2 on v1

v2 whole, which is shorter than its diff:
```python
import functools

import jax
import jax.numpy as jnp
from jax import lax
from jax.experimental import pallas as pl
from jax.experimental.pallas import tpu as pltpu
from jax.sharding import PartitionSpec as P

GROUP = 16
LANES = 128
CHUNKS = 4
SHIFTS = 4
PIECES = 4
CROSS = (3, 5, 7, 9)
PRODUCT = (0, 2, 4, 6)
AHEAD = 2
SPLIT = 4
VMEM_LIMIT = 60 * 1024 * 1024


def shifted(block, axis, distance):
    devices = range(lax.axis_size(axis))
    route = [((i - distance) % len(devices), i) for i in devices]
    return lax.ppermute(block, axis, route)


MESH = pl.DeviceIdType.MESH


def carried_body(mix_ref, env_ref, site_ref, out_ref):
    width, rows, bond = env_ref.shape
    _, states, _, columns = site_ref.shape
    mix = mix_ref[...]
    mix_high = mix.astype(jnp.bfloat16)
    mix_low = (mix - mix_high.astype(jnp.float32)).astype(jnp.bfloat16)
    env = env_ref[...].reshape(width * rows, bond)
    half_done = [
        jnp.dot(env, site_ref[:, t].reshape(bond, columns), preferred_element_type=jnp.float32)
        .reshape(width, rows, columns)
        for t in range(states)
    ]
    dot = functools.partial(jnp.dot, preferred_element_type=jnp.float32)
    step = width // CHUNKS
    for g in range(rows // GROUP):
        span = slice(g * GROUP, (g + 1) * GROUP)
        x = jnp.concatenate(
            [h[:, span].reshape(width * GROUP, columns) for h in half_done], axis=0
        )
        high = x.astype(jnp.bfloat16)
        low = (x - high.astype(jnp.float32)).astype(jnp.bfloat16)
        y = dot(mix_high, high) + dot(mix_high, low) + dot(mix_low, high)
        y = y.astype(jnp.bfloat16).reshape(width, states, GROUP, columns)
        for i in range(CHUNKS):
            out_ref[i, 0, :, :, span, :] = y[i * step : (i + 1) * step]


def greet(parts):
    me = lax.axis_index("sector")
    barrier = pltpu.get_barrier_semaphore()
    for d in range(1, parts):
        pl.semaphore_signal(
            barrier, inc=1, device_id={"sector": lax.rem(me + d, parts)}, device_id_type=MESH
        )
    return barrier


def remote(src, dst, send, recv, target):
    return pltpu.make_async_remote_copy(
        src_ref=src, dst_ref=dst, send_sem=send, recv_sem=recv,
        device_id=target, device_id_type=MESH,
    )


def head_kernel(
    mix_ref, right_hbm, site_hbm, bond_hbm, left_hbm,
    gathered, moved, carried,
    right, bond_ref, blocks, own_site, shift_send, shift_recv, site_send, site_recv,
    block_send, block_recv, local_sem,
):
    parts, states, depth, bond = gathered.shape
    width, rows, _ = right_hbm.shape
    columns = bond // parts
    line = parts // 2
    me = lax.axis_index("sector")
    z, y = me // 2, lax.rem(me, 2)
    regions = lax.axis_size("region")
    region = lax.axis_index("region")
    before = lax.rem(region + regions - 1, regions)
    after = lax.rem(region + 1, regions)
    part_rows = rows // SHIFTS
    piece_columns = bond // PIECES
    twin = 2 * z + 1 - y

    barrier = greet(parts)
    for other in (before, after):
        pl.semaphore_signal(barrier, inc=1, device_id={"region": other}, device_id_type=MESH)
    pl.semaphore_wait(barrier, parts + 1)

    def shift(q):
        span = pl.ds(q * part_rows, part_rows)
        return remote(
            right_hbm.at[:, span], right.at[:, span], shift_send.at[q], shift_recv.at[q],
            {"region": before},
        )

    def cut(piece):
        return pl.ds(pl.multiple_of(piece * piece_columns, piece_columns), piece_columns)

    def hop(way, source, piece, target, first=False):
        there = gathered.at[source, :, :, cut(piece)]
        return remote(
            site_hbm.at[:, :, cut(piece)] if first else there, there,
            site_send.at[way, source, piece], site_recv.at[source, piece], {"sector": target},
        )

    def outward(source, piece, first, ways, act):
        for way in ways:
            there = {0: me + 2, 1: me - 2, 2: twin}[way]
            if way == 2:
                act(hop(way, source, piece, there, first))
            else:
                inside = z + 1 < line if way == 0 else z >= 1

                @pl.when(inside)
                def _():
                    act(hop(way, source, piece, there, first))

    def target_of(d):
        return lax.rem(me + 1 + d, parts)

    def block(q, d):
        return remote(
            blocks.at[q, d], moved.at[q, me], block_send.at[q, d], block_recv.at[q, me],
            {"sector": target_of(d)},
        )

    def block_in(q, d):
        source = target_of(d)
        return remote(
            blocks.at[q, d], moved.at[q, source], block_send.at[q, d], block_recv.at[q, source],
            {"sector": source},
        )

    def own_block(q):
        return pltpu.make_async_copy(
            blocks.at[q, parts - 1], moved.at[q, me], block_send.at[q, parts - 1]
        )

    def start(copy):
        copy.start()

    for q in range(SHIFTS):
        shift(q).start()
    for piece in range(PIECES):
        outward(me, piece, True, (0, 1, 2), start)
    load_bond = pltpu.make_async_copy(bond_hbm, bond_ref, local_sem.at[0])
    load_bond.start()
    load_site = pltpu.make_async_copy(site_hbm, own_site, local_sem.at[1])
    load_site.start()
    load_site.wait()
    keep_site = pltpu.make_async_copy(own_site, gathered.at[me], local_sem.at[1])
    keep_site.start()
    load_bond.wait()

    def product(q):
        shift(q).wait_recv()
        span = pl.ds(q * part_rows, part_rows)
        x = right[:, span].reshape(width * part_rows, bond)

        def step(d, carry):
            j = target_of(d)
            out = lax.dot_general(
                x,
                bond_ref[pl.ds(pl.multiple_of(j * columns, columns), columns), :],
                (((1,), (1,)), ((), ())),
                preferred_element_type=jnp.float32,
            )
            blocks[q, d] = out.astype(jnp.bfloat16).reshape(width, part_rows, columns)
            return carry

        lax.fori_loop(0, parts, step, 0)

    def dispatch(q, cross):
        def step(d, carry):
            same = lax.rem(target_of(d), 2) == y

            @pl.when(jnp.logical_not(same) if cross else same)
            def _():
                block(q, d).start()

            return carry

        lax.fori_loop(0, parts - 1, step, 0)
        if not cross:
            own_block(q).start()

    def relay(distance, piece):
        for way, source in ((0, me - 2 * distance), (1, me + 2 * distance)):
            there = z >= distance if way == 0 else z + distance < line

            @pl.when(there)
            def _():
                hop(way, source, piece, twin).wait_recv()
                outward(source, piece, False, (way, 2), start)

    def tick(i, carry):
        relay(i // PIECES + 1, lax.rem(i, PIECES))
        for q in range(SHIFTS):

            @pl.when(i == PRODUCT[q])
            def _():
                product(q)
                dispatch(q, False)

            @pl.when(i == CROSS[q])
            def _():
                dispatch(q, True)

        return carry

    ticks = (line - 1) * PIECES
    lax.fori_loop(0, ticks, tick, 0)
    keep_site.wait()
    tile = min(rows, LANES)
    per = parts // PIECES

    def absorb(piece, carry):
        for other in range(line):
            hop(2, 2 * other + 1 - y, piece, twin).wait_recv()
        pltpu.emit_pipeline(
            functools.partial(carried_body, mix_ref),
            grid=(rows // tile, per),
            in_specs=[
                pl.BlockSpec((width, tile, bond), lambda i, j: (0, i, 0)),
                pl.BlockSpec((parts, states, depth, columns), lambda i, j: (0, 0, 0, j)),
            ],
            out_specs=[
                pl.BlockSpec(
                    (CHUNKS, 1, width // CHUNKS, states, tile, columns),
                    lambda i, j: (0, j, 0, 0, i, 0),
                )
            ],
        )(
            left_hbm,
            gathered.at[:, :, :, cut(piece)],
            carried.at[:, pl.ds(piece * per, per)],
        )
        return carry

    lax.fori_loop(0, PIECES, absorb, 0)

    def settle(copy):
        copy.wait_send()

    for q in range(SHIFTS):
        shift(q).wait_send()

    def sent(piece, carry):
        outward(me, piece, True, (0, 1, 2), settle)
        return carry

    lax.fori_loop(0, PIECES, sent, 0)

    def relayed(i, carry):
        distance, piece = i // PIECES + 1, lax.rem(i, PIECES)
        for way, source in ((0, me - 2 * distance), (1, me + 2 * distance)):
            there = z >= distance if way == 0 else z + distance < line

            @pl.when(there)
            def _():
                outward(source, piece, False, (way, 2), settle)

        return carry

    lax.fori_loop(0, ticks, relayed, 0)

    def finish(i, carry):
        q, d = i // (parts - 1), lax.rem(i, parts - 1)
        block(q, d).wait_send()
        block_in(q, d).wait_recv()
        return carry

    lax.fori_loop(0, SHIFTS * (parts - 1), finish, 0)
    for q in range(SHIFTS):
        own_block(q).wait()


def head(env_left, site, mpo, env_right, bond_tensor, parts):
    width, rows, bond = env_left.shape
    states, depth, _ = site.shape
    columns = bond // parts
    eye = jnp.eye(GROUP, dtype=jnp.float32)
    side = width * states * GROUP
    mix = jnp.einsum("vwst,ij->wsitvj", mpo, eye, precision=lax.Precision.HIGHEST).reshape(side, side)
    part_rows = rows // SHIFTS
    bf16 = jnp.bfloat16
    anywhere = pl.BlockSpec(memory_space=pl.ANY)
    dma = pltpu.SemaphoreType.DMA
    return pl.pallas_call(
        head_kernel,
        in_specs=[pl.BlockSpec(memory_space=pltpu.VMEM)] + [anywhere] * 4,
        out_specs=[anywhere] * 3,
        out_shape=[
            jax.ShapeDtypeStruct((parts, states, depth, bond), bf16),
            jax.ShapeDtypeStruct((SHIFTS, parts, width, part_rows, columns), bf16),
            jax.ShapeDtypeStruct((CHUNKS, parts, width // CHUNKS, states, rows, columns), bf16),
        ],
        scratch_shapes=[
            pltpu.VMEM((width, rows, bond), bf16),
            pltpu.VMEM((bond, bond), bf16),
            pltpu.VMEM((SHIFTS, parts, width, part_rows, columns), bf16),
            pltpu.VMEM((states, depth, bond), bf16),
            dma((SHIFTS,)),
            dma((SHIFTS,)),
            dma((3, parts, PIECES)),
            dma((parts, PIECES)),
            dma((SHIFTS, parts)),
            dma((SHIFTS, parts)),
            dma((2,)),
        ],
        compiler_params=pltpu.CompilerParams(
            vmem_limit_bytes=VMEM_LIMIT, collective_id=0, has_side_effects=True
        ),
        cost_estimate=pl.CostEstimate(
            flops=3 * width * rows * bond * bond * states,
            bytes_accessed=128 * 1024 * 1024,
            transcendentals=0,
        ),
    )(mix, env_right, site, bond_tensor, env_left)


def rest_kernel(
    gathered, moved, carried,
    env_out, image_out, landed,
    x, turned, env, bond_in, keep, pair_out, pair_in, line_out, line_in, done,
    swap_send, swap_recv, pair_send, pair_recv, line_send, line_recv,
    load_sem, env_sem, out_sem,
):
    parts, states, depth, bond = gathered.shape
    _, _, count, _, _, columns = landed.shape
    width = count * CHUNKS
    part_rows = moved.shape[3]
    line = parts // 2
    group = bond_in.shape[0]
    splits = parts // group
    steps = SHIFTS * splits
    me = lax.axis_index("sector")
    z, y = me // 2, lax.rem(me, 2)
    twin = 2 * z + 1 - y

    pl.semaphore_wait(greet(parts), parts - 1)

    def swap(b, d, receiving=False):
        j = lax.rem(me + 1 + d, parts)
        owner = j if receiving else me
        return remote(
            carried.at[b, j], landed.at[b, owner], swap_send.at[b, d], swap_recv.at[b, owner],
            {"sector": j},
        )

    def dispatch(b):
        def step(d, carry):
            swap(b, d).start()
            return carry

        lax.fori_loop(0, parts - 1, step, 0)

    def fill(b, d):
        n = lax.rem(me + 1 + d, parts)
        return pltpu.make_async_copy(landed.at[b, n], x.at[n], load_sem.at[d])

    def fill_own(b):
        return pltpu.make_async_copy(carried.at[b, me], x.at[me], load_sem.at[parts - 1])

    def turn(n, carry):
        for s in range(states):
            at = pl.multiple_of((n * states + s) * depth, depth)
            for v in range(count):
                turned[v * columns : (v + 1) * columns, pl.ds(at, depth)] = x[n, v, s].T
        return carry

    def env_body(site_ref, out_ref):
        site = site_ref[...].reshape(parts * states * depth, site_ref.shape[-1])
        total = jnp.dot(turned[...], site, preferred_element_type=jnp.float32)
        out_ref[...] = total.astype(jnp.bfloat16).reshape(out_ref.shape)

    def reload(b):
        span = pl.ds(b * count, count)
        return pltpu.make_async_copy(env_out.at[span], env.at[span], env_sem.at[b])

    tile = 2 * LANES
    for b in range(AHEAD):
        dispatch(b)

    def advance(b, carry):
        fill_own(b).start()

        def collect(d, carry):
            swap(b, d, True).wait_recv()
            fill(b, d).start()
            return carry

        lax.fori_loop(0, parts - 1, collect, 0)

        @pl.when(b + AHEAD < CHUNKS)
        def _():
            dispatch(b + AHEAD)

        def filled(d, carry):
            fill(b, d).wait()
            return carry

        lax.fori_loop(0, parts - 1, filled, 0)
        fill_own(b).wait()
        lax.fori_loop(0, parts, turn, 0)
        pltpu.emit_pipeline(
            env_body,
            grid=(bond // tile,),
            in_specs=[pl.BlockSpec((parts, states, depth, tile), lambda j: (0, 0, 0, j))],
            out_specs=[pl.BlockSpec((count, columns, tile), lambda j: (0, 0, j))],
        )(gathered, env_out.at[pl.ds(b * count, count)])
        reload(b).start()
        return carry

    lax.fori_loop(0, CHUNKS, advance, 0)
    for b in range(CHUNKS):
        reload(b).wait()

    def pair_copy(u):
        return remote(
            pair_out.at[u], pair_in.at[u], pair_send.at[u], pair_recv.at[u], {"sector": twin}
        )

    def line_copy(u, t, way):
        slot = t + 1 if way == 0 else t
        return remote(
            line_out.at[u, t], line_in.at[u, slot], line_send.at[u, t], line_recv.at[u, slot],
            {"sector": me + 2 if way == 0 else me - 2},
        )

    def dot(a, b):
        return jnp.dot(a, b, preferred_element_type=jnp.float32)

    def take(u, i):
        q, n = u // splits, lax.rem(u, splits) * group + i
        return pltpu.make_async_copy(
            moved.at[q, n], bond_in.at[i], load_sem.at[i]
        )

    def image(u):
        for i in range(group):
            take(u, i).start()
        for i in range(group):
            take(u, i).wait()
        left = jnp.concatenate(
            [bond_in[:, w].reshape(group * part_rows, columns) for w in range(width)], axis=1
        )

        def right(j):
            at = pl.multiple_of(j * columns, columns)
            return env[:, :, pl.ds(at, columns)].reshape(width * columns, columns)

        for t in range(line):
            pair_out[u, t] = dot(left, right(2 * t + 1 - y)).astype(jnp.bfloat16)
        for t in range(line):
            keep[u, t] = dot(left, right(2 * t + y))
        pair_copy(u).start()

    def paired(u):
        pair_copy(u).wait_recv()
        keep[u] = keep[u] + pair_in[u].astype(jnp.float32)

    def relay(s, way):
        first = z if way == 0 else line - 1 - z
        u = s - 1 - first
        live = jnp.logical_and(u >= 0, u < steps)
        for t in range(line):
            sends = jnp.logical_and(live, t > z if way == 0 else t < z)

            @pl.when(jnp.logical_and(sends, first == 0))
            def _():
                line_out[u, t] = keep[u, t].astype(jnp.bfloat16)

            @pl.when(jnp.logical_and(sends, first > 0))
            def _():
                slot = t + 1 if way == 0 else t
                line_copy(u, t, way).wait_recv()
                line_out[u, t] = (
                    keep[u, t] + line_in[u, slot].astype(jnp.float32)
                ).astype(jnp.bfloat16)

    def send_on(s, way):
        first = z if way == 0 else line - 1 - z
        u = s - 1 - first
        live = jnp.logical_and(u >= 0, u < steps)
        for t in range(line):

            @pl.when(jnp.logical_and(live, t > z if way == 0 else t < z))
            def _():
                line_copy(u, t, way).start()

    def result(u):
        return pltpu.make_async_copy(done.at[u], image_out.at[u], out_sem.at[u])

    def total(u):
        @pl.when(z > 0)
        def _():
            line_copy(u, z, 0).wait_recv()
            keep[u, z] = keep[u, z] + line_in[u, z + 1].astype(jnp.float32)

        @pl.when(z < line - 1)
        def _():
            line_copy(u, z, 1).wait_recv()
            keep[u, z] = keep[u, z] + line_in[u, z].astype(jnp.float32)

        done[u] = keep[u, z].astype(jnp.bfloat16)

    def pass_on(s, carry):
        @pl.when(s < steps)
        def _():
            image(s)

        @pl.when(jnp.logical_and(s >= 1, s <= steps))
        def _():
            paired(s - 1)

        relay(s, 0)
        relay(s, 1)

        @pl.when(s >= line)
        def _():
            total(s - line)

        send_on(s, 0)
        send_on(s, 1)

        @pl.when(s >= line)
        def _():
            result(s - line).start()

        return carry

    lax.fori_loop(0, steps + line, pass_on, 0)

    def sent(b, carry):
        def step(d, carry):
            swap(b, d).wait_send()
            return carry

        return lax.fori_loop(0, parts - 1, step, carry)

    lax.fori_loop(0, CHUNKS, sent, 0)

    def ended(u, carry):
        pair_copy(u).wait_send()
        result(u).wait()
        for t in range(line):
            @pl.when(t > z)
            def _():
                line_copy(u, t, 0).wait_send()

            @pl.when(t < z)
            def _():
                line_copy(u, t, 1).wait_send()

        return carry

    lax.fori_loop(0, steps, ended, 0)


def rest_of(gathered, moved, carried):
    parts, states, depth, bond = gathered.shape
    _, _, count, _, _, columns = carried.shape
    width = count * CHUNKS
    part_rows = moved.shape[3]
    line = parts // 2
    group = max(parts // SPLIT, 1)
    steps = SHIFTS * (parts // group)
    block = (group * part_rows, columns)
    anywhere = pl.BlockSpec(memory_space=pl.ANY)
    dma = pltpu.SemaphoreType.DMA
    bf16 = jnp.bfloat16
    return pl.pallas_call(
        rest_kernel,
        in_specs=[anywhere] * 3,
        out_specs=[anywhere] * 3,
        out_shape=[
            jax.ShapeDtypeStruct((width, columns, bond), bf16),
            jax.ShapeDtypeStruct((steps,) + block, bf16),
            jax.ShapeDtypeStruct(carried.shape, bf16),
        ],
        scratch_shapes=[
            pltpu.VMEM(carried.shape[1:], bf16),
            pltpu.VMEM((count * columns, parts * states * depth), bf16),
            pltpu.VMEM((width, columns, bond), bf16),
            pltpu.VMEM((group, width, part_rows, columns), bf16),
            pltpu.VMEM((steps, line) + block, jnp.float32),
            pltpu.VMEM((steps, line) + block, bf16),
            pltpu.VMEM((steps, line) + block, bf16),
            pltpu.VMEM((steps, line) + block, bf16),
            pltpu.VMEM((steps, line + 1) + block, bf16),
            pltpu.VMEM((steps,) + block, bf16),
            dma((CHUNKS, parts)),
            dma((CHUNKS, parts)),
            dma((steps,)),
            dma((steps,)),
            dma((steps, line)),
            dma((steps, line + 1)),
            dma((parts,)),
            dma((CHUNKS,)),
            dma((steps,)),
        ],
        compiler_params=pltpu.CompilerParams(
            vmem_limit_bytes=VMEM_LIMIT, collective_id=1, has_side_effects=True
        ),
        cost_estimate=pl.CostEstimate(
            flops=3 * width * columns * parts * states * depth * bond,
            bytes_accessed=128 * 1024 * 1024,
            transcendentals=0,
        ),
    )(gathered, moved, carried)


def local(env_left, site_tensor, mpo_tensor, env_right, bond_tensor):
    parts = lax.axis_size("sector")
    _, rows, bond = env_left.shape[1:]
    columns = bond // parts
    gathered, moved, carried = head(
        env_left[0], site_tensor[0].transpose(1, 0, 2), mpo_tensor[0],
        env_right[0], bond_tensor[0], parts,
    )
    env_new, image, _ = rest_of(gathered, moved, carried)
    image_rows = (
        image.reshape(SHIFTS, parts, rows // SHIFTS, columns)
        .transpose(3, 1, 0, 2)
        .reshape(columns, bond)
    )
    return (env_new[None], image_rows[None])


def plain_local(env_left, site_tensor, mpo_tensor, env_right, bond_tensor):
    width = env_left.shape[1]
    states = site_tensor.shape[2]
    gathered = lax.all_gather(site_tensor, "sector", axis=1, tiled=True)[0]
    half_done = jnp.einsum(
        "wak,ksc->wasc", env_left[0], gathered, preferred_element_type=jnp.float32
    )
    carried = jnp.einsum(
        "vwst,vatc->wsac", mpo_tensor[0], half_done, precision=lax.Precision.HIGHEST
    ).astype(jnp.bfloat16)
    carried = carried.reshape((width * states,) + carried.shape[2:])
    right_next = shifted(env_right, "region", -1)[0]
    bond_right = jnp.einsum(
        "wbc,kc->wbk", right_next, bond_tensor[0], preferred_element_type=jnp.float32
    ).astype(jnp.bfloat16)
    carried_moved = lax.all_to_all(carried, "sector", split_axis=2, concat_axis=1, tiled=True)
    bond_moved = lax.all_to_all(bond_right, "sector", split_axis=2, concat_axis=1, tiled=True)
    carried_moved = carried_moved.reshape((width, states) + carried_moved.shape[1:])
    env_new = jnp.einsum(
        "wsac,asb->wcb", carried_moved, gathered, preferred_element_type=jnp.float32
    ).astype(jnp.bfloat16)
    image_rows = lax.psum_scatter(
        jnp.einsum("wka,wbk->ab", env_new, bond_moved, preferred_element_type=jnp.float32),
        "sector",
        scatter_dimension=0,
        tiled=True,
    )
    return (env_new[None], image_rows.astype(jnp.bfloat16)[None])


def solution(mesh):
    def body(env_left, site_tensor, mpo_tensor, env_right, bond_tensor):
        width, rows, bond = env_left.shape[1:]
        columns = bond // mesh.shape["sector"]
        tiled = rows % LANES == 0 and columns % LANES == 0 and width % CHUNKS == 0 and rows % (16 * SHIFTS) == 0
        tiled = tiled and mesh.shape["sector"] % 2 == 0 and mesh.shape["region"] > 2
        step = local if tiled else plain_local
        return step(env_left, site_tensor, mpo_tensor, env_right, bond_tensor)

    return jax.shard_map(
        body,
        mesh=mesh,
        in_specs=(
            P("region", None, "sector", None),
            P("region", "sector", None, None),
            P("region", None, None, None, None),
            P("region", None, "sector", None),
            P("region", None, None),
        ),
        out_specs=(P("region", None, "sector", None), P("region", "sector", None)),
        check_vma=False,
    )
```

time: 870 us -> 845 us (0.971); the launches traced: 859 us -> 843 us
  Pallas kernels: 840 us -> 825 us
    pallas_call x1, Pallas kernels: 552 us -> 491 us  [rest_of(): pl.pallas_call(rest_kernel, in_specs=[anywhere] * 3, out_specs=[anywhere]...]
    pallas_call x1, Pallas kernels: 288 us -> 334 us  [head(): pl.pallas_call(head_kernel, in_specs=[pl.BlockSpec(memory_space=pltpu.VME...]
where the time goes in v2:
time: 845 us; the launch traced here: 843 us
  Pallas kernels  825 us (98%)
  local copies, waits for them, and re-layouts  17.3 us (2%)
    pallas_call x1, Pallas kernels, rest_of(): pl.pallas_call(rest_kernel, in_specs=[anywhere] * 3, out_specs=[anywhere]...  491 us
    pallas_call x1, Pallas kernels, head(): pl.pallas_call(head_kernel, in_specs=[pl.BlockSpec(memory_space=pltpu.VME...  334 us

profile of v2, /device:TPU:0, one launch (start us, length us, event | category | flops | bytes accessed | tf_op | source)
XLA Modules:
  0.0 843.0 jit_solution(13187221354531590710)
XLA Ops:
  0.6 0.8 copy.10
  1.4 0.2 multiply_bitcast_fusion
  1.7 1.5 reshape.10.mix_ref
  3.2 3.8 copy.15
  7.0 333.9 %shard_map.68 = (bf16[8,2,256,2048]{3,2,1,0:T(8,128)(2,1)}, bf16[4,8,8,64,256]{4,3,2,1,0:T(8,128)(2,1)}, bf16[4,8,2,2,256,256]{5,4,3,2,1,0:T(8,128)(2,1)}) custom-call(f32[256,256]{1,0:T(8,128)} %reshape.10.mix_ref, bf16[8,256,2048]{2,1,0:T(8,128)(2,1)} %bitcast.23, bf16[2,256,2048]{2,1,0:T(8,128)(2,1)} %bitcast.20, bf16[2048,2048]{1,0:T(8,128)(2,1)} %bitcast.24, ...), custom_call_target="tpu_custom_call" | custom-call | flops 51539607552 | bytes 134217728 | tf_op jit(solution)/shard_map/pallas_call | solution.py:300
  340.9 490.9 %shard_map.69 = (bf16[8,256,2048]{2,1,0:T(8,128)(2,1)}, bf16[16,128,256]{2,1,0:T(8,128)(2,1)}, bf16[4,8,2,2,256,256]{5,4,3,2,1,0:T(8,128)(2,1)}) custom-call(bf16[8,2,256,2048]{3,2,1,0:T(8,128)(2,1)} %get-tuple-element.7.gathered, bf16[4,8,8,64,256]{4,3,2,1,0:T(8,128)(2,1)} %get-tuple-element.8.moved, bf16[4,8,2,2,256,256]{5,4,3,2,1,0:T(8,128)(2,1)} %get-tuple-element.9.carried), custom_call_target="tpu_custom_call" | custom-call | flops 51539607552 | bytes 134217728 | tf_op jit(solution)/shard_map/pallas_call | solution.py:584
  831.8 1.3 copy.12
  833.1 1.4 copy.13
  834.5 8.4 %copy.17 = bf16[1,8,256,2048]{3,2,1,0:T(8,128)(2,1)} copy(bf16[1,8,256,2048]{3,2,1,0:T(8,128)(2,1)} %bitcast.18) | data formatting | bytes 16777216
  (1 shorter events, 0.0 us)

commit v3 on v2

--- a/solution.py
+++ b/solution.py
@@ -9,12 +9,13 @@
 
 GROUP = 16
 LANES = 128
-CHUNKS = 4
+HALVES = 2
+CHUNKS = 2
 SHIFTS = 4
-PIECES = 4
-CROSS = (3, 5, 7, 9)
-PRODUCT = (0, 2, 4, 6)
-AHEAD = 2
+CROSS = (4, 6, 11, 12)
+PRODUCT = (0, 1, 2, 3)
+OWN_LATER = 2
+ABSORB = 7
 SPLIT = 4
 VMEM_LIMIT = 60 * 1024 * 1024
 
@@ -28,31 +29,41 @@
 MESH = pl.DeviceIdType.MESH
 
 
-def carried_body(mix_ref, env_ref, site_ref, out_ref):
+def carried_into(mix_ref, env_ref, site_ref, out_ref):
     width, rows, bond = env_ref.shape
     _, states, _, columns = site_ref.shape
+    sub = columns // 2
+    tile = min(rows, LANES)
     mix = mix_ref[...]
     mix_high = mix.astype(jnp.bfloat16)
     mix_low = (mix - mix_high.astype(jnp.float32)).astype(jnp.bfloat16)
-    env = env_ref[...].reshape(width * rows, bond)
-    half_done = [
-        jnp.dot(env, site_ref[:, t].reshape(bond, columns), preferred_element_type=jnp.float32)
-        .reshape(width, rows, columns)
-        for t in range(states)
-    ]
     dot = functools.partial(jnp.dot, preferred_element_type=jnp.float32)
     step = width // CHUNKS
-    for g in range(rows // GROUP):
-        span = slice(g * GROUP, (g + 1) * GROUP)
-        x = jnp.concatenate(
-            [h[:, span].reshape(width * GROUP, columns) for h in half_done], axis=0
-        )
-        high = x.astype(jnp.bfloat16)
-        low = (x - high.astype(jnp.float32)).astype(jnp.bfloat16)
-        y = dot(mix_high, high) + dot(mix_high, low) + dot(mix_low, high)
-        y = y.astype(jnp.bfloat16).reshape(width, states, GROUP, columns)
-        for i in range(CHUNKS):
-            out_ref[i, 0, :, :, span, :] = y[i * step : (i + 1) * step]
+
+    def rows_of(i, carry):
+        top = pl.multiple_of(i * tile, tile)
+        env = env_ref[:, pl.ds(top, tile)].reshape(width * tile, bond)
+        half_done = [
+            dot(env, site_ref[:, t].reshape(bond, columns)).reshape(width, tile, columns)
+            for t in range(states)
+        ]
+        for g in range(tile // GROUP):
+            span = slice(g * GROUP, (g + 1) * GROUP)
+            x = jnp.concatenate(
+                [h[:, span].reshape(width * GROUP, columns) for h in half_done], axis=0
+            )
+            high = x.astype(jnp.bfloat16)
+            low = (x - high.astype(jnp.float32)).astype(jnp.bfloat16)
+            y = dot(mix_high, high) + dot(mix_high, low) + dot(mix_low, high)
+            y = y.astype(jnp.bfloat16).reshape(width, states, GROUP, columns)
+            for i in range(CHUNKS):
+                for j in range(2):
+                    out_ref[i, j, :, :, pl.ds(top + g * GROUP, GROUP), :] = y[
+                        i * step : (i + 1) * step, :, :, j * sub : (j + 1) * sub
+                    ]
+        return carry
+
+    lax.fori_loop(0, rows // tile, rows_of, 0)
 
 
 def greet(parts):
@@ -74,12 +85,13 @@
 
 def head_kernel(
     mix_ref, right_hbm, site_hbm, bond_hbm, left_hbm,
-    gathered, moved, carried,
-    right, bond_ref, blocks, own_site, shift_send, shift_recv, site_send, site_recv,
-    block_send, block_recv, local_sem,
+    gathered, moved, landed, carried,
+    right, bond_ref, blocks, left, tiles, outs,
+    shift_send, shift_recv, site_send, site_recv,
+    block_send, block_recv, swap_send, swap_recv, out_sem, tile_sem, local_sem,
 ):
-    parts, states, depth, bond = gathered.shape
-    width, rows, _ = right_hbm.shape
+    _, parts, states, _, _ = gathered.shape
+    width, rows, bond = right_hbm.shape
     columns = bond // parts
     line = parts // 2
     me = lax.axis_index("sector")
@@ -89,7 +101,6 @@
     before = lax.rem(region + regions - 1, regions)
     after = lax.rem(region + 1, regions)
     part_rows = rows // SHIFTS
-    piece_columns = bond // PIECES
     twin = 2 * z + 1 - y
 
     barrier = greet(parts)
@@ -104,27 +115,24 @@
             {"region": before},
         )
 
-    def cut(piece):
-        return pl.ds(pl.multiple_of(piece * piece_columns, piece_columns), piece_columns)
-
-    def hop(way, source, piece, target, first=False):
-        there = gathered.at[source, :, :, cut(piece)]
+    def hop(way, source, p, t, target, first=False):
+        there = gathered.at[p, source, t]
         return remote(
-            site_hbm.at[:, :, cut(piece)] if first else there, there,
-            site_send.at[way, source, piece], site_recv.at[source, piece], {"sector": target},
-        )
-
-    def outward(source, piece, first, ways, act):
+            site_hbm.at[p, t] if first else there, there,
+            site_send.at[way, p, source, t], site_recv.at[p, source, t], {"sector": target},
+        )
+
+    def outward(source, p, t, first, ways, act):
         for way in ways:
             there = {0: me + 2, 1: me - 2, 2: twin}[way]
             if way == 2:
-                act(hop(way, source, piece, there, first))
+                act(hop(way, source, p, t, there, first))
             else:
                 inside = z + 1 < line if way == 0 else z >= 1
 
                 @pl.when(inside)
                 def _():
-                    act(hop(way, source, piece, there, first))
+                    act(hop(way, source, p, t, there, first))
 
     def target_of(d):
         return lax.rem(me + 1 + d, parts)
@@ -150,17 +158,23 @@
     def start(copy):
         copy.start()
 
+    def settle(copy):
+        copy.wait_send()
+
     for q in range(SHIFTS):
         shift(q).start()
-    for piece in range(PIECES):
-        outward(me, piece, True, (0, 1, 2), start)
+    for t in range(states):
+        outward(me, 0, t, True, (0, 1, 2), start)
     load_bond = pltpu.make_async_copy(bond_hbm, bond_ref, local_sem.at[0])
     load_bond.start()
-    load_site = pltpu.make_async_copy(site_hbm, own_site, local_sem.at[1])
-    load_site.start()
-    load_site.wait()
-    keep_site = pltpu.make_async_copy(own_site, gathered.at[me], local_sem.at[1])
-    keep_site.start()
+    load_left = pltpu.make_async_copy(left_hbm, left, local_sem.at[1])
+    load_left.start()
+    keep_site = [
+        pltpu.make_async_copy(site_hbm.at[p], gathered.at[p, me], local_sem.at[2 + p])
+        for p in range(HALVES)
+    ]
+    for copy in keep_site:
+        copy.start()
     load_bond.wait()
 
     def product(q):
@@ -195,17 +209,117 @@
         if not cross:
             own_block(q).start()
 
-    def relay(distance, piece):
+    hops = (line - 1) * states
+    ticks = HALVES * hops
+
+    def relayed(i, act, receive):
+        p, distance, t = i // hops, lax.rem(i, hops) // states + 1, lax.rem(i, states)
         for way, source in ((0, me - 2 * distance), (1, me + 2 * distance)):
             there = z >= distance if way == 0 else z + distance < line
 
             @pl.when(there)
             def _():
-                hop(way, source, piece, twin).wait_recv()
-                outward(source, piece, False, (way, 2), start)
+                if receive:
+                    hop(way, source, p, t, twin).wait_recv()
+                outward(source, p, t, False, (way, 2), act)
+
+    def tile_copies(a):
+        p, slot = a // line, lax.rem(a, 2)
+        m = lax.rem(z + 1 + a, line)
+        span = pl.ds(pl.multiple_of(m * columns, columns), columns)
+        mine = pltpu.make_async_copy(
+            site_hbm.at[p, :, :, span], tiles.at[slot, me], tile_sem.at[slot, parts - 1]
+        )
+        return mine, lambda d: pltpu.make_async_copy(
+            gathered.at[p, target_of(d), :, :, span], tiles.at[slot, target_of(d)],
+            tile_sem.at[slot, d],
+        )
+
+    def each(count, act):
+        def step(d, carry):
+            act(d)
+            return carry
+
+        lax.fori_loop(0, count, step, 0)
+
+    def load_tile(a):
+        mine, other = tile_copies(a)
+        mine.start()
+        each(parts - 1, lambda d: other(d).start())
+
+    def have_tile(a):
+        mine, other = tile_copies(a)
+        mine.wait()
+        each(parts - 1, lambda d: other(d).wait())
+
+    def swap(a, i, j):
+        to = 2 * lax.rem(z + 1 + a, line) + j
+        return to, remote(
+            outs.at[a, i, j], landed.at[i, me], swap_send.at[i, to], swap_recv.at[i, me],
+            {"sector": to},
+        ), pltpu.make_async_copy(outs.at[a, i, j], landed.at[i, me], swap_send.at[i, to])
+
+    def store(a, i, j):
+        to = 2 * lax.rem(z + 1 + a, line) + j
+        slot = lax.rem(a, 2)
+        return pltpu.make_async_copy(
+            outs.at[line + slot, i, j], carried.at[i, to], out_sem.at[slot, i, j]
+        )
+
+    def absorb(a):
+        p = a // line
+
+        @pl.when(lax.rem(a, line) == 0)
+        def _():
+            for other in range(line):
+                for t in range(states):
+                    hop(2, 2 * other + 1 - y, p, t, twin).wait_recv()
+            load_tile(a)
+
+        have_tile(a)
+
+        @pl.when(lax.rem(a, line) < line - 1)
+        def _():
+            load_tile(a + 1)
+
+        @pl.when(a >= line + 2)
+        def _():
+            for i in range(CHUNKS):
+                for j in range(2):
+                    store(a - 2, i, j).wait()
+
+        slot = jnp.where(p == 0, a, line + lax.rem(a, 2))
+        carried_into(mix_ref, left, tiles.at[lax.rem(a, 2)], outs.at[slot])
+        for i in range(CHUNKS):
+            for j in range(2):
+
+                @pl.when(p == 0)
+                def _():
+                    to, far, near = swap(a, i, j)
+
+                    @pl.when(to == me)
+                    def _():
+                        near.start()
+
+                    @pl.when(to != me)
+                    def _():
+                        far.start()
+
+                @pl.when(p > 0)
+                def _():
+                    store(a, i, j).start()
 
     def tick(i, carry):
-        relay(i // PIECES + 1, lax.rem(i, PIECES))
+        @pl.when(i < ticks)
+        def _():
+            relayed(i, start, True)
+
+        @pl.when(i == OWN_LATER)
+        def _():
+            for p in range(1, HALVES):
+                for t in range(states):
+                    outward(me, p, t, True, (0, 1, 2), start)
+
         for q in range(SHIFTS):
 
             @pl.when(i == PRODUCT[q])
@@ -217,107 +331,102 @@
             def _():
                 dispatch(q, True)
 
+        @pl.when(i == ABSORB)
+        def _():
+            load_left.wait()
+
+        early = jnp.logical_and(i >= ABSORB, i < ABSORB + line)
+
+        @pl.when(jnp.logical_or(early, i >= ticks))
+        def _():
+            absorb(jnp.where(i >= ticks, i - ticks + line, i - ABSORB))
+
         return carry
 
-    ticks = (line - 1) * PIECES
-    lax.fori_loop(0, ticks, tick, 0)
-    keep_site.wait()
-    tile = min(rows, LANES)
-    per = parts // PIECES
-
-    def absorb(piece, carry):
-        for other in range(line):
-            hop(2, 2 * other + 1 - y, piece, twin).wait_recv()
-        pltpu.emit_pipeline(
-            functools.partial(carried_body, mix_ref),
-            grid=(rows // tile, per),
-            in_specs=[
-                pl.BlockSpec((width, tile, bond), lambda i, j: (0, i, 0)),
-                pl.BlockSpec((parts, states, depth, columns), lambda i, j: (0, 0, 0, j)),
-            ],
-            out_specs=[
-                pl.BlockSpec(
-                    (CHUNKS, 1, width // CHUNKS, states, tile, columns),
-                    lambda i, j: (0, j, 0, 0, i, 0),
-                )
-            ],
-        )(
-            left_hbm,
-            gathered.at[:, :, :, cut(piece)],
-            carried.at[:, pl.ds(piece * per, per)],
-        )
-        return carry
-
-    lax.fori_loop(0, PIECES, absorb, 0)
-
-    def settle(copy):
-        copy.wait_send()
-
+    lax.fori_loop(0, ticks + line, tick, 0)
+
+    for copy in keep_site:
+        copy.wait()
     for q in range(SHIFTS):
         shift(q).wait_send()
-
-    def sent(piece, carry):
-        outward(me, piece, True, (0, 1, 2), settle)
-        return carry
-
-    lax.fori_loop(0, PIECES, sent, 0)
-
-    def relayed(i, carry):
-        distance, piece = i // PIECES + 1, lax.rem(i, PIECES)
-        for way, source in ((0, me - 2 * distance), (1, me + 2 * distance)):
-            there = z >= distance if way == 0 else z + distance < line
-
-            @pl.when(there)
-            def _():
-                outward(source, piece, False, (way, 2), settle)
-
-        return carry
-
-    lax.fori_loop(0, ticks, relayed, 0)
-
-    def finish(i, carry):
+    for p in range(HALVES):
+        for t in range(states):
+            outward(me, p, t, True, (0, 1, 2), settle)
+    each(ticks, lambda i: relayed(i, settle, False))
+
+    def finish(i):
         q, d = i // (parts - 1), lax.rem(i, parts - 1)
         block(q, d).wait_send()
         block_in(q, d).wait_recv()
-        return carry
-
-    lax.fori_loop(0, SHIFTS * (parts - 1), finish, 0)
+
+    each(SHIFTS * (parts - 1), finish)
     for q in range(SHIFTS):
         own_block(q).wait()
 
+    def swapped(a):
+        for i in range(CHUNKS):
+            for j in range(2):
+                to, far, near = swap(a, i, j)
+
+                @pl.when(to == me)
+                def _():
+                    near.wait()
+
+                @pl.when(to != me)
+                def _():
+                    far.wait_send()
+                    remote(
+                        outs.at[a, i, j], landed.at[i, to], swap_send.at[i, to],
+                        swap_recv.at[i, to], {"sector": to},
+                    ).wait_recv()
+
+    each(line, swapped)
+    for a in range(2 * line - 2, 2 * line):
+        for i in range(CHUNKS):
+            for j in range(2):
+                store(a, i, j).wait()
+
 
 def head(env_left, site, mpo, env_right, bond_tensor, parts):
     width, rows, bond = env_left.shape
-    states, depth, _ = site.shape
+    _, states, depth, _ = site.shape
     columns = bond // parts
     eye = jnp.eye(GROUP, dtype=jnp.float32)
     side = width * states * GROUP
     mix = jnp.einsum("vwst,ij->wsitvj", mpo, eye, precision=lax.Precision.HIGHEST).reshape(side, side)
     part_rows = rows // SHIFTS
+    carried = (width // CHUNKS, states, rows, columns // HALVES)
     bf16 = jnp.bfloat16
     anywhere = pl.BlockSpec(memory_space=pl.ANY)
     dma = pltpu.SemaphoreType.DMA
     return pl.pallas_call(
         head_kernel,
         in_specs=[pl.BlockSpec(memory_space=pltpu.VMEM)] + [anywhere] * 4,
-        out_specs=[anywhere] * 3,
+        out_specs=[anywhere] * 4,
         out_shape=[
-            jax.ShapeDtypeStruct((parts, states, depth, bond), bf16),
+            jax.ShapeDtypeStruct((HALVES, parts, states, depth, bond // HALVES), bf16),
             jax.ShapeDtypeStruct((SHIFTS, parts, width, part_rows, columns), bf16),
-            jax.ShapeDtypeStruct((CHUNKS, parts, width // CHUNKS, states, rows, columns), bf16),
+            jax.ShapeDtypeStruct((CHUNKS, parts) + carried, bf16),
+            jax.ShapeDtypeStruct((CHUNKS, parts) + carried, bf16),
         ],
         scratch_shapes=[
             pltpu.VMEM((width, rows, bond), bf16),
             pltpu.VMEM((bond, bond), bf16),
             pltpu.VMEM((SHIFTS, parts, width, part_rows, columns), bf16),
-            pltpu.VMEM((states, depth, bond), bf16),
+            pltpu.VMEM((width, rows, bond), bf16),
+            pltpu.VMEM((2, parts, states, depth, columns), bf16),
+            pltpu.VMEM((parts // 2 + 2, CHUNKS, 2) + carried, bf16),
             dma((SHIFTS,)),
             dma((SHIFTS,)),
-            dma((3, parts, PIECES)),
-            dma((parts, PIECES)),
+            dma((3, HALVES, parts, states)),
+            dma((HALVES, parts, states)),
             dma((SHIFTS, parts)),
             dma((SHIFTS, parts)),
-            dma((2,)),
+            dma((CHUNKS, parts)),
+            dma((CHUNKS, parts)),
+            dma((2, CHUNKS, 2)),
+            dma((2, parts)),
+            dma((2 + HALVES,)),
         ],
         compiler_params=pltpu.CompilerParams(
             vmem_limit_bytes=VMEM_LIMIT, collective_id=0, has_side_effects=True
@@ -331,15 +440,15 @@
 
 
 def rest_kernel(
-    gathered, moved, carried,
+    gathered, moved, landed_first, carried,
     env_out, image_out, landed,
     x, turned, env, bond_in, keep, pair_out, pair_in, line_out, line_in, done,
     swap_send, swap_recv, pair_send, pair_recv, line_send, line_recv,
     load_sem, env_sem, out_sem,
 ):
-    parts, states, depth, bond = gathered.shape
-    _, _, count, _, _, columns = landed.shape
-    width = count * CHUNKS
+    _, parts, states, depth, _ = gathered.shape
+    _, _, count, _, _, sub = landed.shape
+    width, columns, bond = env_out.shape
     part_rows = moved.shape[3]
     line = parts // 2
     group = bond_in.shape[0]
@@ -366,66 +475,91 @@
 
         lax.fori_loop(0, parts - 1, step, 0)
 
-    def fill(b, d):
+    def fill(b, d, first):
         n = lax.rem(me + 1 + d, parts)
-        return pltpu.make_async_copy(landed.at[b, n], x.at[n], load_sem.at[d])
-
-    def fill_own(b):
-        return pltpu.make_async_copy(carried.at[b, me], x.at[me], load_sem.at[parts - 1])
+        origin = landed_first if first else landed
+        return pltpu.make_async_copy(origin.at[b, n], x.at[n], load_sem.at[d])
+
+    def fill_own(b, first):
+        origin = landed_first if first else carried
+        return pltpu.make_async_copy(origin.at[b, me], x.at[me], load_sem.at[parts - 1])
 
     def turn(n, carry):
         for s in range(states):
             at = pl.multiple_of((n * states + s) * depth, depth)
             for v in range(count):
-                turned[v * columns : (v + 1) * columns, pl.ds(at, depth)] = x[n, v, s].T
+                turned[v * sub : (v + 1) * sub, pl.ds(at, depth)] = x[n, v, s].T
         return carry
 
-    def env_body(site_ref, out_ref):
-        site = site_ref[...].reshape(parts * states * depth, site_ref.shape[-1])
-        total = jnp.dot(turned[...], site, preferred_element_type=jnp.float32)
-        out_ref[...] = total.astype(jnp.bfloat16).reshape(out_ref.shape)
-
-    def reload(b):
-        span = pl.ds(b * count, count)
-        return pltpu.make_async_copy(env_out.at[span], env.at[span], env_sem.at[b])
+    def env_body(*refs):
+        out_ref = refs[-1]
+        tile = out_ref.shape[-1]
+        totals = []
+        for site_ref in refs[:-1]:
+            site = site_ref[0].reshape(parts * states * depth, site_ref.shape[-1])
+            totals.append(
+                jnp.dot(turned[...], site, preferred_element_type=jnp.float32)
+                .astype(jnp.bfloat16)
+                .reshape(count, sub, site_ref.shape[-1])
+            )
+        for k in range(tile // sub):
+            piece = slice(k // HALVES * sub, (k // HALVES + 1) * sub)
+            out_ref[:, :, k * sub : (k + 1) * sub] = totals[k % HALVES][:, :, piece]
+
+    def spot(ref, i):
+        p, b = i // CHUNKS, lax.rem(i, CHUNKS)
+        return ref.at[
+            pl.ds(b * count, count), pl.ds(pl.multiple_of(p * sub, sub), sub)
+        ]
+
+    def reload(i):
+        return pltpu.make_async_copy(spot(env_out, i), spot(env, i), env_sem.at[i])
 
     tile = 2 * LANES
-    for b in range(AHEAD):
+    for b in range(CHUNKS):
         dispatch(b)
 
-    def advance(b, carry):
-        fill_own(b).start()
-
-        def collect(d, carry):
-            swap(b, d, True).wait_recv()
-            fill(b, d).start()
+    def advance(i, carry):
+        b = lax.rem(i, CHUNKS)
+        for first in (True, False):
+
+            @pl.when(i < CHUNKS if first else i >= CHUNKS)
+            def _():
+                fill_own(b, first).start()
+
+                def collect(d, carry):
+                    if not first:
+                        swap(b, d, True).wait_recv()
+                    fill(b, d, first).start()
+                    return carry
+
+                lax.fori_loop(0, parts - 1, collect, 0)
+
+        def filled(d, carry):
+            fill(b, d, True).wait()
             return carry
 
-        lax.fori_loop(0, parts - 1, collect, 0)
-
-        @pl.when(b + AHEAD < CHUNKS)
-        def _():
-            dispatch(b + AHEAD)
-
-        def filled(d, carry):
-            fill(b, d).wait()
-            return carry
-
         lax.fori_loop(0, parts - 1, filled, 0)
-        fill_own(b).wait()
+        fill_own(b, True).wait()
         lax.fori_loop(0, parts, turn, 0)
         pltpu.emit_pipeline(
             env_body,
-            grid=(bond // tile,),
-            in_specs=[pl.BlockSpec((parts, states, depth, tile), lambda j: (0, 0, 0, j))],
-            out_specs=[pl.BlockSpec((count, columns, tile), lambda j: (0, 0, j))],
-        )(gathered, env_out.at[pl.ds(b * count, count)])
-        reload(b).start()
+            grid=(bond // (tile * HALVES),),
+            in_specs=[
+                pl.BlockSpec(
+                    (1, parts, states, depth, tile),
+                    functools.partial(lambda p, j: (p, 0, 0, 0, j), p),
+                )
+                for p in range(HALVES)
+            ],
+            out_specs=[pl.BlockSpec((count, sub, tile * HALVES), lambda j: (0, 0, j))],
+        )(*[gathered] * HALVES, spot(env_out, i))
+        reload(i).start()
         return carry
 
-    lax.fori_loop(0, CHUNKS, advance, 0)
-    for b in range(CHUNKS):
-        reload(b).wait()
+    lax.fori_loop(0, HALVES * CHUNKS, advance, 0)
+    for i in range(HALVES * CHUNKS):
+        reload(i).wait()
 
     def pair_copy(u):
         return remote(
@@ -569,10 +703,11 @@
     lax.fori_loop(0, steps, ended, 0)
 
 
-def rest_of(gathered, moved, carried):
-    parts, states, depth, bond = gathered.shape
-    _, _, count, _, _, columns = carried.shape
-    width = count * CHUNKS
+def rest_of(gathered, moved, landed, carried):
+    _, parts, states, depth, _ = gathered.shape
+    _, _, count, _, _, sub = carried.shape
+    width, columns = count * CHUNKS, sub * HALVES
+    bond = parts * columns
     part_rows = moved.shape[3]
     line = parts // 2
     group = max(parts // SPLIT, 1)
@@ -583,7 +718,7 @@
     bf16 = jnp.bfloat16
     return pl.pallas_call(
         rest_kernel,
-        in_specs=[anywhere] * 3,
+        in_specs=[anywhere] * 4,
         out_specs=[anywhere] * 3,
         out_shape=[
             jax.ShapeDtypeStruct((width, columns, bond), bf16),
@@ -592,7 +727,7 @@
         ],
         scratch_shapes=[
             pltpu.VMEM(carried.shape[1:], bf16),
-            pltpu.VMEM((count * columns, parts * states * depth), bf16),
+            pltpu.VMEM((count * sub, parts * states * depth), bf16),
             pltpu.VMEM((width, columns, bond), bf16),
             pltpu.VMEM((group, width, part_rows, columns), bf16),
             pltpu.VMEM((steps, line) + block, jnp.float32),
@@ -608,7 +743,7 @@
             dma((steps, line)),
             dma((steps, line + 1)),
             dma((parts,)),
-            dma((CHUNKS,)),
+            dma((HALVES * CHUNKS,)),
             dma((steps,)),
         ],
         compiler_params=pltpu.CompilerParams(
@@ -619,18 +754,19 @@
             bytes_accessed=128 * 1024 * 1024,
             transcendentals=0,
         ),
-    )(gathered, moved, carried)
+    )(gathered, moved, landed, carried)
 
 
 def local(env_left, site_tensor, mpo_tensor, env_right, bond_tensor):
     parts = lax.axis_size("sector")
     _, rows, bond = env_left.shape[1:]
     columns = bond // parts
-    gathered, moved, carried = head(
-        env_left[0], site_tensor[0].transpose(1, 0, 2), mpo_tensor[0],
-        env_right[0], bond_tensor[0], parts,
+    site = site_tensor[0].reshape(rows, -1, parts, HALVES, columns // HALVES)
+    site = site.transpose(3, 1, 0, 2, 4).reshape(HALVES, -1, rows, bond // HALVES)
+    gathered, moved, landed, carried = head(
+        env_left[0], site, mpo_tensor[0], env_right[0], bond_tensor[0], parts,
     )
-    env_new, image, _ = rest_of(gathered, moved, carried)
+    env_new, image, _ = rest_of(gathered, moved, landed, carried)
     image_rows = (
         image.reshape(SHIFTS, parts, rows // SHIFTS, columns)
         .transpose(3, 1, 0, 2)
@@ -673,7 +809,7 @@
     def body(env_left, site_tensor, mpo_tensor, env_right, bond_tensor):
         width, rows, bond = env_left.shape[1:]
         columns = bond // mesh.shape["sector"]
-        tiled = rows % LANES == 0 and columns % LANES == 0 and width % CHUNKS == 0 and rows % (16 * SHIFTS) == 0
+        tiled = rows % LANES == 0 and columns % (HALVES * LANES) == 0 and width % CHUNKS == 0 and rows % (16 * SHIFTS) == 0
         tiled = tiled and mesh.shape["sector"] % 2 == 0 and mesh.shape["region"] > 2
         step = local if tiled else plain_local
         return step(env_left, site_tensor, mpo_tensor, env_right, bond_tensor)

time: 845 us -> 803 us (0.950)
  Pallas kernels: 825 us -> 779 us
    pallas_call x1, Pallas kernels: 491 us -> 310 us  [rest_of(): pl.pallas_call(rest_kernel, in_specs=[anywhere] * 4, out_specs=[anywhere]...]
    pallas_call x1, Pallas kernels: 334 us -> 469 us  [head(): pl.pallas_call(head_kernel, in_specs=[pl.BlockSpec(memory_space=pltpu.VME...]
where the time goes in v3:
time: 803 us; the launch traced here: 802 us
  Pallas kernels  779 us (97%)
  local copies, waits for them, and re-layouts  22 us (3%)
    pallas_call x1, Pallas kernels, head(): pl.pallas_call(head_kernel, in_specs=[pl.BlockSpec(memory_space=pltpu.VME...  469 us
    pallas_call x1, Pallas kernels, rest_of(): pl.pallas_call(rest_kernel, in_specs=[anywhere] * 4, out_specs=[anywhere]...  310 us

profile of v3, /device:TPU:0, one launch (start us, length us, event | category | flops | bytes accessed | tf_op | source)
XLA Modules:
  0.0 802.1 jit_solution(8449631593092031233)
XLA Ops:
  0.6 0.8 copy.10
  1.4 0.2 multiply_bitcast_fusion
  1.7 1.5 reshape.13.mix_ref
  3.2 4.4 reshape_squeeze.3
  7.6 1.9 copy.15
  9.4 2.3 reshape.14.site_hbm
  11.7 469.3 %shard_map.68 = (bf16[2,8,2,256,1024]{4,3,2,1,0:T(8,128)(2,1)}, bf16[4,8,8,64,256]{4,3,2,1,0:T(8,128)(2,1)}, bf16[2,8,4,2,256,128]{5,4,3,2,1,0:T(8,128)(2,1)}, bf16[2,8,4,2,256,128]{5,4,3,2,1,0:T(8,128)(2,1)}) custom-call(f32[256,256]{1,0:T(8,128)} %reshape.13.mix_ref, bf16[8,256,2048]{2,1,0:T(8,128)(2,1)} %bitcast.23, ...), custom_call_target="tpu_custom_call" | custom-call | flops 51539607552 | bytes 134217728 | tf_op jit(solution)/shard_map/pallas_call | solution.py:402
  481.1 309.9 %shard_map.69 = (bf16[8,256,2048]{2,1,0:T(8,128)(2,1)}, bf16[16,128,256]{2,1,0:T(8,128)(2,1)}, bf16[2,8,4,2,256,128]{5,4,3,2,1,0:T(8,128)(2,1)}) custom-call(bf16[2,8,2,256,1024]{4,3,2,1,0:T(8,128)(2,1)} %get-tuple-element.8.gathered, bf16[4,8,8,64,256]{4,3,2,1,0:T(8,128)(2,1)} %get-tuple-element.9.moved, ...), custom_call_target="tpu_custom_call" | custom-call | flops 51539607552 | bytes 134217728 | tf_op jit(solution)/shard_map/pallas_call | solution.py:719
  791.0 1.3 copy.12
  792.2 1.4 copy.13
  793.7 8.4 %copy.17 = bf16[1,8,256,2048]{3,2,1,0:T(8,128)(2,1)} copy(bf16[1,8,256,2048]{3,2,1,0:T(8,128)(2,1)} %bitcast.18) | data formatting | bytes 16777216
  (1 shorter events, 0.0 us)

commit v4 on v3

--- a/solution.py
+++ b/solution.py
@@ -10,7 +10,10 @@
 GROUP = 16
 LANES = 128
 HALVES = 2
-CHUNKS = 2
+CHUNKS = 4
+LATE_FROM = 0
+AHEAD = 4
+LATE_AFTER = 5
 SHIFTS = 4
 CROSS = (4, 6, 11, 12)
 PRODUCT = (0, 1, 2, 3)
@@ -66,6 +69,16 @@
     lax.fori_loop(0, rows // tile, rows_of, 0)
 
 
+def inner(parts, device):
+    z = device // 2
+    return jnp.logical_and(z > 0, z < parts // 2 - 1)
+
+
+def waits(parts, source, target, q):
+    same = lax.rem(source + target, 2) == 0
+    return jnp.logical_and(jnp.logical_and(same, inner(parts, source)), q >= LATE_FROM)
+
+
 def greet(parts):
     me = lax.axis_index("sector")
     barrier = pltpu.get_barrier_semaphore()
@@ -85,11 +98,12 @@
 
 def head_kernel(
     mix_ref, right_hbm, site_hbm, bond_hbm, left_hbm,
-    gathered, moved, landed, carried,
+    gathered, moved, landed, carried, late,
     right, bond_ref, blocks, left, tiles, outs,
     shift_send, shift_recv, site_send, site_recv,
     block_send, block_recv, swap_send, swap_recv, out_sem, tile_sem, local_sem,
 ):
+
     _, parts, states, _, _ = gathered.shape
     width, rows, bond = right_hbm.shape
     columns = bond // parts
@@ -148,6 +162,14 @@
         return remote(
             blocks.at[q, d], moved.at[q, source], block_send.at[q, d], block_recv.at[q, source],
             {"sector": source},
+        )
+
+    def held(q, d):
+        return waits(parts, me, target_of(d), q)
+
+    def put_off(q, d):
+        return pltpu.make_async_copy(
+            blocks.at[q, d], late.at[q, target_of(d) // 2], block_send.at[q, d]
         )
 
     def own_block(q):
@@ -199,9 +221,15 @@
         def step(d, carry):
             same = lax.rem(target_of(d), 2) == y
 
-            @pl.when(jnp.logical_not(same) if cross else same)
+            @pl.when(jnp.logical_not(same) if cross else jnp.logical_and(same, jnp.logical_not(held(q, d))))
             def _():
                 block(q, d).start()
+
+            if not cross:
+
+                @pl.when(held(q, d))
+                def _():
+                    put_off(q, d).start()
 
             return carry
 
@@ -356,8 +384,18 @@
 
     def finish(i):
         q, d = i // (parts - 1), lax.rem(i, parts - 1)
-        block(q, d).wait_send()
-        block_in(q, d).wait_recv()
+
+        @pl.when(held(q, d))
+        def _():
+            put_off(q, d).wait()
+
+        @pl.when(jnp.logical_not(held(q, d)))
+        def _():
+            block(q, d).wait_send()
+
+        @pl.when(jnp.logical_not(waits(parts, target_of(d), me, q)))
+        def _():
+            block_in(q, d).wait_recv()
 
     each(SHIFTS * (parts - 1), finish)
     for q in range(SHIFTS):
@@ -402,12 +440,13 @@
     return pl.pallas_call(
         head_kernel,
         in_specs=[pl.BlockSpec(memory_space=pltpu.VMEM)] + [anywhere] * 4,
-        out_specs=[anywhere] * 4,
+        out_specs=[anywhere] * 5,
         out_shape=[
             jax.ShapeDtypeStruct((HALVES, parts, states, depth, bond // HALVES), bf16),
             jax.ShapeDtypeStruct((SHIFTS, parts, width, part_rows, columns), bf16),
             jax.ShapeDtypeStruct((CHUNKS, parts) + carried, bf16),
             jax.ShapeDtypeStruct((CHUNKS, parts) + carried, bf16),
+            jax.ShapeDtypeStruct((SHIFTS, parts // 2, width, part_rows, columns), bf16),
         ],
         scratch_shapes=[
             pltpu.VMEM((width, rows, bond), bf16),
@@ -440,10 +479,10 @@
 
 
 def rest_kernel(
-    gathered, moved, landed_first, carried,
-    env_out, image_out, landed,
+    gathered, moved_before, landed_first, carried, late,
+    env_out, image_out, landed, moved,
     x, turned, env, bond_in, keep, pair_out, pair_in, line_out, line_in, done,
-    swap_send, swap_recv, pair_send, pair_recv, line_send, line_recv,
+    swap_send, swap_recv, late_send, late_recv, pair_send, pair_recv, line_send, line_recv,
     load_sem, env_sem, out_sem,
 ):
     _, parts, states, depth, _ = gathered.shape
@@ -515,8 +554,25 @@
     def reload(i):
         return pltpu.make_async_copy(spot(env_out, i), spot(env, i), env_sem.at[i])
 
+    def late_block(q, k, receiving=False):
+        to = lax.rem(z + 1 + k, line)
+        other = 2 * to + y
+        owner = other if receiving else me
+        return remote(
+            late.at[q, to], moved.at[q, owner], late_send.at[q, k],
+            late_recv.at[q, owner // 2], {"sector": other},
+        )
+
+    def late_blocks(q, act, receiving=False):
+        for k in range(line - 1):
+            other = 2 * lax.rem(z + 1 + k, line) + y
+
+            @pl.when(waits(parts, other, me, q) if receiving else waits(parts, me, other, q))
+            def _():
+                act(late_block(q, k, receiving))
+
     tile = 2 * LANES
-    for b in range(CHUNKS):
+    for b in range(min(AHEAD, CHUNKS)):
         dispatch(b)
 
     def advance(i, carry):
@@ -534,6 +590,15 @@
                     return carry
 
                 lax.fori_loop(0, parts - 1, collect, 0)
+
+        @pl.when(jnp.logical_and(i >= CHUNKS, b + AHEAD < CHUNKS))
+        def _():
+            dispatch(b + AHEAD)
+
+        @pl.when(i == LATE_AFTER)
+        def _():
+            for q in range(SHIFTS):
+                late_blocks(q, lambda copy: copy.start())
 
         def filled(d, carry):
             fill(b, d, True).wait()
@@ -653,6 +718,10 @@
     def pass_on(s, carry):
         @pl.when(s < steps)
         def _():
+            @pl.when(lax.rem(s, splits) == 0)
+            def _():
+                late_blocks(s // splits, lambda copy: copy.wait_recv(), True)
+
             image(s)
 
         @pl.when(jnp.logical_and(s >= 1, s <= steps))
@@ -685,6 +754,9 @@
         return lax.fori_loop(0, parts - 1, step, carry)
 
     lax.fori_loop(0, CHUNKS, sent, 0)
+
+    for q in range(SHIFTS):
+        late_blocks(q, lambda copy: copy.wait_send())
 
     def ended(u, carry):
         pair_copy(u).wait_send()
@@ -703,7 +775,7 @@
     lax.fori_loop(0, steps, ended, 0)
 
 
-def rest_of(gathered, moved, landed, carried):
+def rest_of(gathered, moved, landed, carried, late):
     _, parts, states, depth, _ = gathered.shape
     _, _, count, _, _, sub = carried.shape
     width, columns = count * CHUNKS, sub * HALVES
@@ -718,12 +790,14 @@
     bf16 = jnp.bfloat16
     return pl.pallas_call(
         rest_kernel,
-        in_specs=[anywhere] * 4,
-        out_specs=[anywhere] * 3,
+        in_specs=[anywhere] * 5,
+        out_specs=[anywhere] * 4,
+        input_output_aliases={1: 3},
         out_shape=[
             jax.ShapeDtypeStruct((width, columns, bond), bf16),
             jax.ShapeDtypeStruct((steps,) + block, bf16),
             jax.ShapeDtypeStruct(carried.shape, bf16),
+            jax.ShapeDtypeStruct(moved.shape, bf16),
         ],
         scratch_shapes=[
             pltpu.VMEM(carried.shape[1:], bf16),
@@ -738,6 +812,8 @@
             pltpu.VMEM((steps,) + block, bf16),
             dma((CHUNKS, parts)),
             dma((CHUNKS, parts)),
+            dma((SHIFTS, line)),
+            dma((SHIFTS, line)),
             dma((steps,)),
             dma((steps,)),
             dma((steps, line)),
@@ -754,7 +830,7 @@
             bytes_accessed=128 * 1024 * 1024,
             transcendentals=0,
         ),
-    )(gathered, moved, landed, carried)
+    )(gathered, moved, landed, carried, late)
 
 
 def local(env_left, site_tensor, mpo_tensor, env_right, bond_tensor):
@@ -763,10 +839,10 @@
     columns = bond // parts
     site = site_tensor[0].reshape(rows, -1, parts, HALVES, columns // HALVES)
     site = site.transpose(3, 1, 0, 2, 4).reshape(HALVES, -1, rows, bond // HALVES)
-    gathered, moved, landed, carried = head(
+    gathered, moved, landed, carried, late = head(
         env_left[0], site, mpo_tensor[0], env_right[0], bond_tensor[0], parts,
     )
-    env_new, image, _ = rest_of(gathered, moved, landed, carried)
+    env_new, image, *_ = rest_of(gathered, moved, landed, carried, late)
     image_rows = (
         image.reshape(SHIFTS, parts, rows // SHIFTS, columns)
         .transpose(3, 1, 0, 2)

time: 803 us -> 761 us (0.948)
  Pallas kernels: 779 us -> 737 us
    pallas_call x1, Pallas kernels: 469 us -> 417 us  [head(): pl.pallas_call(head_kernel, in_specs=[pl.BlockSpec(memory_space=pltpu.VME...]
    pallas_call x1, Pallas kernels: 310 us -> 320 us  [rest_of(): pl.pallas_call(rest_kernel, in_specs=[anywhere] * 5, out_specs=[anywhere]...]
where the time goes in v4:
time: 761 us; the launch traced here: 760 us
  Pallas kernels  737 us (97%)
  local copies, waits for them, and re-layouts  22 us (3%)
    pallas_call x1, Pallas kernels, head(): pl.pallas_call(head_kernel, in_specs=[pl.BlockSpec(memory_space=pltpu.VME...  417 us
    pallas_call x1, Pallas kernels, rest_of(): pl.pallas_call(rest_kernel, in_specs=[anywhere] * 5, out_specs=[anywhere]...  320 us

profile of v4, /device:TPU:0, one launch (start us, length us, event | category | flops | bytes accessed | tf_op | source)
XLA Modules:
  0.0 759.6 jit_solution(9191197962758770237)
XLA Ops:
  0.6 0.8 copy.11
  1.4 0.2 multiply_bitcast_fusion
  1.7 1.5 reshape.13.mix_ref
  3.2 4.4 reshape_squeeze.3
  7.6 1.9 copy.16
  9.4 2.3 reshape.14.site_hbm
  11.7 416.7 %shard_map.68 = (bf16[2,8,2,256,1024]{4,3,2,1,0:T(8,128)(2,1)}, bf16[4,8,8,64,256]{4,3,2,1,0:T(8,128)(2,1)}, bf16[4,8,2,2,256,128]{5,4,3,2,1,0:T(8,128)(2,1)}, b...) custom-call(f32[256,256]{1,0:T(8,128)} %reshape.13.mix_ref, bf16[8,256,2048]{2,1,0:T(8,128)(2,1)} %bitcast.23, ...), custom_call_target="tpu_custom_call" | custom-call | flops 51539607552 | bytes 134217728 | tf_op jit(solution)/shard_map/pallas_call | solution.py:440
  428.4 320.0 %shard_map.69 = (bf16[8,256,2048]{2,1,0:T(8,128)(2,1)}, bf16[16,128,256]{2,1,0:T(8,128)(2,1)}, bf16[4,8,2,2,256,128]{5,4,3,2,1,0:T(8,128)(2,1)}, bf16[4,8,8,64,256]{4,3,2,1,0:T(8,128)(2,1)}) custom-call(bf16[2,8,2,256,1024]{4,3,2,1,0:T(8,128)(2,1)} %get-tuple-element.9.gathered, ...), custom_call_target="tpu_custom_call", output_to_operand_aliasing={{3}: (1, {})} | custom-call | flops 51539607552 | bytes 134217728 | tf_op jit(solution)/shard_map/pallas_call | solution.py:791
  748.4 1.3 copy.13
  749.7 1.4 copy.14
  751.2 8.4 %copy.19 = bf16[1,8,256,2048]{3,2,1,0:T(8,128)(2,1)} copy(bf16[1,8,256,2048]{3,2,1,0:T(8,128)(2,1)} %bitcast.18) | data formatting | bytes 16777216
  (1 shorter events, 0.0 us)

commit v5 on v4

--- a/solution.py
+++ b/solution.py
@@ -11,15 +11,17 @@
 LANES = 128
 HALVES = 2
 CHUNKS = 4
-LATE_FROM = 0
+EDGE_FROM = 2
 AHEAD = 4
-LATE_AFTER = 5
+LATE_AFTER = 7
 SHIFTS = 4
 CROSS = (4, 6, 11, 12)
 PRODUCT = (0, 1, 2, 3)
 OWN_LATER = 2
 ABSORB = 7
 SPLIT = 4
+LAG = 2
+HOP = 2
 VMEM_LIMIT = 60 * 1024 * 1024
 
 
@@ -76,7 +78,7 @@
 
 def waits(parts, source, target, q):
     same = lax.rem(source + target, 2) == 0
-    return jnp.logical_and(jnp.logical_and(same, inner(parts, source)), q >= LATE_FROM)
+    return jnp.logical_and(same, jnp.logical_or(inner(parts, source), q >= EDGE_FROM))
 
 
 def greet(parts):
@@ -490,7 +492,7 @@
     width, columns, bond = env_out.shape
     part_rows = moved.shape[3]
     line = parts // 2
-    group = bond_in.shape[0]
+    group = bond_in.shape[1]
     splits = parts // group
     steps = SHIFTS * splits
     me = lax.axis_index("sector")
@@ -642,18 +644,33 @@
         return jnp.dot(a, b, preferred_element_type=jnp.float32)
 
     def take(u, i):
-        q, n = u // splits, lax.rem(u, splits) * group + i
+        q, n, slot = u // splits, lax.rem(u, splits) * group + i, lax.rem(u, 2)
         return pltpu.make_async_copy(
-            moved.at[q, n], bond_in.at[i], load_sem.at[i]
-        )
+            moved.at[q, n], bond_in.at[slot, i], load_sem.at[slot * group + i]
+        )
+
+    def fetch(u):
+        @pl.when(lax.rem(u, splits) == 0)
+        def _():
+            late_blocks(u // splits, lambda copy: copy.wait_recv(), True)
+
+        for i in range(group):
+            take(u, i).start()
 
     def image(u):
         for i in range(group):
-            take(u, i).start()
-        for i in range(group):
             take(u, i).wait()
+
+        @pl.when(u + 1 < steps)
+        def _():
+            fetch(u + 1)
+
         left = jnp.concatenate(
-            [bond_in[:, w].reshape(group * part_rows, columns) for w in range(width)], axis=1
+            [
+                bond_in[lax.rem(u, 2), :, w].reshape(group * part_rows, columns)
+                for w in range(width)
+            ],
+            axis=1,
         )
 
         def right(j):
@@ -672,7 +689,7 @@
 
     def relay(s, way):
         first = z if way == 0 else line - 1 - z
-        u = s - 1 - first
+        u = s - LAG - HOP * first
         live = jnp.logical_and(u >= 0, u < steps)
         for t in range(line):
             sends = jnp.logical_and(live, t > z if way == 0 else t < z)
@@ -691,7 +708,7 @@
 
     def send_on(s, way):
         first = z if way == 0 else line - 1 - z
-        u = s - 1 - first
+        u = s - LAG - HOP * first
         live = jnp.logical_and(u >= 0, u < steps)
         for t in range(line):
 
@@ -715,36 +732,35 @@
 
         done[u] = keep[u, z].astype(jnp.bfloat16)
 
+    last = LAG + HOP * (line - 2) + 1
+
     def pass_on(s, carry):
         @pl.when(s < steps)
         def _():
-            @pl.when(lax.rem(s, splits) == 0)
-            def _():
-                late_blocks(s // splits, lambda copy: copy.wait_recv(), True)
-
             image(s)
 
-        @pl.when(jnp.logical_and(s >= 1, s <= steps))
-        def _():
-            paired(s - 1)
+        @pl.when(jnp.logical_and(s >= LAG, s < steps + LAG))
+        def _():
+            paired(s - LAG)
 
         relay(s, 0)
         relay(s, 1)
 
-        @pl.when(s >= line)
-        def _():
-            total(s - line)
+        @pl.when(s >= last)
+        def _():
+            total(s - last)
 
         send_on(s, 0)
         send_on(s, 1)
 
-        @pl.when(s >= line)
-        def _():
-            result(s - line).start()
+        @pl.when(s >= last)
+        def _():
+            result(s - last).start()
 
         return carry
 
-    lax.fori_loop(0, steps + line, pass_on, 0)
+    fetch(0)
+    lax.fori_loop(0, steps + last, pass_on, 0)
 
     def sent(b, carry):
         def step(d, carry):
@@ -803,7 +819,7 @@
             pltpu.VMEM(carried.shape[1:], bf16),
             pltpu.VMEM((count * sub, parts * states * depth), bf16),
             pltpu.VMEM((width, columns, bond), bf16),
-            pltpu.VMEM((group, width, part_rows, columns), bf16),
+            pltpu.VMEM((2, group, width, part_rows, columns), bf16),
             pltpu.VMEM((steps, line) + block, jnp.float32),
             pltpu.VMEM((steps, line) + block, bf16),
             pltpu.VMEM((steps, line) + block, bf16),

time: 761 us -> 744 us (0.978)
  Pallas kernels: 737 us -> 715 us
    pallas_call x1, Pallas kernels: 417 us -> 389 us  [head(): pl.pallas_call(head_kernel, in_specs=[pl.BlockSpec(memory_space=pltpu.VME...]
where the time goes in v5:
time: 744 us; the launch traced here: 738 us
  Pallas kernels  715 us (96%)
  local copies, waits for them, and re-layouts  22 us (3%)
    pallas_call x1, Pallas kernels, head(): pl.pallas_call(head_kernel, in_specs=[pl.BlockSpec(memory_space=pltpu.VME...  389 us
    pallas_call x1, Pallas kernels, rest_of(): pl.pallas_call(rest_kernel, in_specs=[anywhere] * 5, out_specs=[anywhere]...  327 us

profile of v5, /device:TPU:0, one launch (start us, length us, event | category | flops | bytes accessed | tf_op | source)
XLA Modules:
  0.0 738.4 jit_solution(14305554300362648426)
XLA Ops:
  0.6 0.8 copy.11
  1.4 0.2 multiply_bitcast_fusion
  1.7 1.5 reshape.13.mix_ref
  3.2 4.4 reshape_squeeze.3
  7.6 1.9 copy.16
  9.4 2.3 reshape.14.site_hbm
  11.7 388.8 %shard_map.68 = (bf16[2,8,2,256,1024]{4,3,2,1,0:T(8,128)(2,1)}, bf16[4,8,8,64,256]{4,3,2,1,0:T(8,128)(2,1)}, bf16[4,8,2,2,256,128]{5,4,3,2,1,0:T(8,128)(2,1)}, b...) custom-call(f32[256,256]{1,0:T(8,128)} %reshape.13.mix_ref, bf16[8,256,2048]{2,1,0:T(8,128)(2,1)} %bitcast.23, ...), custom_call_target="tpu_custom_call" | custom-call | flops 51539607552 | bytes 134217728 | tf_op jit(solution)/shard_map/pallas_call | solution.py:442
  400.6 326.6 %shard_map.69 = (bf16[8,256,2048]{2,1,0:T(8,128)(2,1)}, bf16[16,128,256]{2,1,0:T(8,128)(2,1)}, bf16[4,8,2,2,256,128]{5,4,3,2,1,0:T(8,128)(2,1)}, bf16[4,8,8,64,256]{4,3,2,1,0:T(8,128)(2,1)}) custom-call(bf16[2,8,2,256,1024]{4,3,2,1,0:T(8,128)(2,1)} %get-tuple-element.9.gathered, ...), custom_call_target="tpu_custom_call", output_to_operand_aliasing={{3}: (1, {})} | custom-call | flops 51539607552 | bytes 134217728 | tf_op jit(solution)/shard_map/pallas_call | solution.py:807
  727.2 1.3 copy.13
  728.5 1.4 copy.14
  729.9 8.4 %copy.19 = bf16[1,8,256,2048]{3,2,1,0:T(8,128)(2,1)} copy(bf16[1,8,256,2048]{3,2,1,0:T(8,128)(2,1)} %bitcast.18) | data formatting | bytes 16777216
  (1 shorter events, 0.0 us)

commit v6 on v5

--- a/solution.py
+++ b/solution.py
@@ -101,9 +101,9 @@
 def head_kernel(
     mix_ref, right_hbm, site_hbm, bond_hbm, left_hbm,
     gathered, moved, landed, carried, late,
-    right, bond_ref, blocks, left, tiles, outs,
+    right, bond_ref, blocks, left, tiles, outs, own,
     shift_send, shift_recv, site_send, site_recv,
-    block_send, block_recv, swap_send, swap_recv, out_sem, tile_sem, local_sem,
+    block_send, block_recv, swap_send, swap_recv, out_sem, tile_sem, local_sem, own_sem,
 ):
 
     _, parts, states, _, _ = gathered.shape
@@ -122,7 +122,6 @@
     barrier = greet(parts)
     for other in (before, after):
         pl.semaphore_signal(barrier, inc=1, device_id={"region": other}, device_id_type=MESH)
-    pl.semaphore_wait(barrier, parts + 1)
 
     def shift(q):
         span = pl.ds(q * part_rows, part_rows)
@@ -134,7 +133,7 @@
     def hop(way, source, p, t, target, first=False):
         there = gathered.at[p, source, t]
         return remote(
-            site_hbm.at[p, t] if first else there, there,
+            own.at[p, t] if first else there, there,
             site_send.at[way, p, source, t], site_recv.at[p, source, t], {"sector": target},
         )
 
@@ -185,16 +184,34 @@
     def settle(copy):
         copy.wait_send()
 
+    sub = columns // HALVES
+
+    def sort_site(p, j):
+        return pltpu.make_async_copy(
+            site_hbm.at[:, :, pl.ds(j * columns + p * sub, sub)],
+            own.at[p, :, :, pl.ds(j * sub, sub)],
+            own_sem.at[p, j],
+        )
+
+    for p in range(HALVES):
+        for j in range(parts):
+            sort_site(p, j).start()
+    pl.semaphore_wait(barrier, parts + 1)
     for q in range(SHIFTS):
         shift(q).start()
+    for j in range(parts):
+        sort_site(0, j).wait()
     for t in range(states):
         outward(me, 0, t, True, (0, 1, 2), start)
+    for p in range(1, HALVES):
+        for j in range(parts):
+            sort_site(p, j).wait()
     load_bond = pltpu.make_async_copy(bond_hbm, bond_ref, local_sem.at[0])
     load_bond.start()
     load_left = pltpu.make_async_copy(left_hbm, left, local_sem.at[1])
     load_left.start()
     keep_site = [
-        pltpu.make_async_copy(site_hbm.at[p], gathered.at[p, me], local_sem.at[2 + p])
+        pltpu.make_async_copy(own.at[p], gathered.at[p, me], local_sem.at[2 + p])
         for p in range(HALVES)
     ]
     for copy in keep_site:
@@ -258,7 +275,7 @@
         m = lax.rem(z + 1 + a, line)
         span = pl.ds(pl.multiple_of(m * columns, columns), columns)
         mine = pltpu.make_async_copy(
-            site_hbm.at[p, :, :, span], tiles.at[slot, me], tile_sem.at[slot, parts - 1]
+            own.at[p, :, :, span], tiles.at[slot, me], tile_sem.at[slot, parts - 1]
         )
         return mine, lambda d: pltpu.make_async_copy(
             gathered.at[p, target_of(d), :, :, span], tiles.at[slot, target_of(d)],
@@ -429,7 +446,7 @@
 
 def head(env_left, site, mpo, env_right, bond_tensor, parts):
     width, rows, bond = env_left.shape
-    _, states, depth, _ = site.shape
+    states, depth, _ = site.shape
     columns = bond // parts
     eye = jnp.eye(GROUP, dtype=jnp.float32)
     side = width * states * GROUP
@@ -457,6 +474,7 @@
             pltpu.VMEM((width, rows, bond), bf16),
             pltpu.VMEM((2, parts, states, depth, columns), bf16),
             pltpu.VMEM((parts // 2 + 2, CHUNKS, 2) + carried, bf16),
+            pltpu.VMEM((HALVES, states, depth, bond // HALVES), bf16),
             dma((SHIFTS,)),
             dma((SHIFTS,)),
             dma((3, HALVES, parts, states)),
@@ -468,6 +486,7 @@
             dma((2, CHUNKS, 2)),
             dma((2, parts)),
             dma((2 + HALVES,)),
+            dma((HALVES, parts)),
         ],
         compiler_params=pltpu.CompilerParams(
             vmem_limit_bytes=VMEM_LIMIT, collective_id=0, has_side_effects=True
@@ -853,8 +872,7 @@
     parts = lax.axis_size("sector")
     _, rows, bond = env_left.shape[1:]
     columns = bond // parts
-    site = site_tensor[0].reshape(rows, -1, parts, HALVES, columns // HALVES)
-    site = site.transpose(3, 1, 0, 2, 4).reshape(HALVES, -1, rows, bond // HALVES)
+    site = site_tensor[0].transpose(1, 0, 2)
     gathered, moved, landed, carried, late = head(
         env_left[0], site, mpo_tensor[0], env_right[0], bond_tensor[0], parts,
     )

time: 744 us -> 740 us (level)
  no operation moved by 1% of the time
where the time goes in v6:
time: 740 us
  Pallas kernels  722 us (98%)
  local copies, waits for them, and re-layouts  17.3 us (2%)
    pallas_call x1, Pallas kernels, head(): pl.pallas_call(head_kernel, in_specs=[pl.BlockSpec(memory_space=pltpu.VME...  388 us
    pallas_call x1, Pallas kernels, rest_of(): pl.pallas_call(rest_kernel, in_specs=[anywhere] * 5, out_specs=[anywhere]...  333 us

profile of v6, /device:TPU:0, one launch (start us, length us, event | category | flops | bytes accessed | tf_op | source)
XLA Modules:
  0.0 739.8 jit_solution(17516158492766433684)
XLA Ops:
  0.6 0.8 copy.11
  1.4 0.2 multiply_bitcast_fusion
  1.7 1.5 reshape.10.mix_ref
  3.2 3.8 copy.16
  7.0 388.2 %shard_map.68 = (bf16[2,8,2,256,1024]{4,3,2,1,0:T(8,128)(2,1)}, bf16[4,8,8,64,256]{4,3,2,1,0:T(8,128)(2,1)}, bf16[4,8,2,2,256,128]{5,4,3,2,1,0:T(8,128)(2,1)}, b...) custom-call(f32[256,256]{1,0:T(8,128)} %reshape.10.mix_ref, bf16[8,256,2048]{2,1,0:T(8,128)(2,1)} %bitcast.23, ...), custom_call_target="tpu_custom_call" | custom-call | flops 51539607552 | bytes 134217728 | tf_op jit(solution)/shard_map/pallas_call | solution.py:459
  395.2 333.4 %shard_map.69 = (bf16[8,256,2048]{2,1,0:T(8,128)(2,1)}, bf16[16,128,256]{2,1,0:T(8,128)(2,1)}, bf16[4,8,2,2,256,128]{5,4,3,2,1,0:T(8,128)(2,1)}, bf16[4,8,8,64,256]{4,3,2,1,0:T(8,128)(2,1)}) custom-call(bf16[2,8,2,256,1024]{4,3,2,1,0:T(8,128)(2,1)} %get-tuple-element.9.gathered, ...), custom_call_target="tpu_custom_call", output_to_operand_aliasing={{3}: (1, {})} | custom-call | flops 51539607552 | bytes 134217728 | tf_op jit(solution)/shard_map/pallas_call | solution.py:826
  728.6 1.3 copy.13
  729.9 1.4 copy.14
  731.4 8.4 %copy.19 = bf16[1,8,256,2048]{3,2,1,0:T(8,128)(2,1)} copy(bf16[1,8,256,2048]{3,2,1,0:T(8,128)(2,1)} %bitcast.18) | data formatting | bytes 16777216
  (1 shorter events, 0.0 us)

commit v7 on v6

--- a/solution.py
+++ b/solution.py
@@ -618,7 +618,7 @@
 
         @pl.when(i == LATE_AFTER)
         def _():
-            for q in range(SHIFTS):
+            for q in range(2):
                 late_blocks(q, lambda copy: copy.start())
 
         def filled(d, carry):
@@ -754,6 +754,12 @@
     last = LAG + HOP * (line - 2) + 1
 
     def pass_on(s, carry):
+        for q in range(2, SHIFTS):
+
+            @pl.when(s == (q - 2) * splits + 1)
+            def _():
+                late_blocks(q, lambda copy: copy.start())
+
         @pl.when(s < steps)
         def _():
             image(s)

time: 740 us -> 737 us (level)
  no operation moved by 1% of the time
where the time goes in v7:
time: 737 us; the launch traced here: 736 us
  Pallas kernels  718 us (97%)
  local copies, waits for them, and re-layouts  17.3 us (2%)
    pallas_call x1, Pallas kernels, head(): pl.pallas_call(head_kernel, in_specs=[pl.BlockSpec(memory_space=pltpu.VME...  388 us
    pallas_call x1, Pallas kernels, rest_of(): pl.pallas_call(rest_kernel, in_specs=[anywhere] * 5, out_specs=[anywhere]...  330 us

profile of v7, /device:TPU:0, one launch (start us, length us, event | category | flops | bytes accessed | tf_op | source)
XLA Modules:
  0.0 735.9 jit_solution(9216009021444613791)
XLA Ops:
  0.6 0.8 copy.11
  1.4 0.2 multiply_bitcast_fusion
  1.7 1.5 reshape.10.mix_ref
  3.2 3.8 copy.16
  7.0 388.2 %shard_map.68 = (bf16[2,8,2,256,1024]{4,3,2,1,0:T(8,128)(2,1)}, bf16[4,8,8,64,256]{4,3,2,1,0:T(8,128)(2,1)}, bf16[4,8,2,2,256,128]{5,4,3,2,1,0:T(8,128)(2,1)}, b...) custom-call(f32[256,256]{1,0:T(8,128)} %reshape.10.mix_ref, bf16[8,256,2048]{2,1,0:T(8,128)(2,1)} %bitcast.23, ...), custom_call_target="tpu_custom_call" | custom-call | flops 51539607552 | bytes 134217728 | tf_op jit(solution)/shard_map/pallas_call | solution.py:459
  395.2 329.6 %shard_map.69 = (bf16[8,256,2048]{2,1,0:T(8,128)(2,1)}, bf16[16,128,256]{2,1,0:T(8,128)(2,1)}, bf16[4,8,2,2,256,128]{5,4,3,2,1,0:T(8,128)(2,1)}, bf16[4,8,8,64,256]{4,3,2,1,0:T(8,128)(2,1)}) custom-call(bf16[2,8,2,256,1024]{4,3,2,1,0:T(8,128)(2,1)} %get-tuple-element.9.gathered, ...), custom_call_target="tpu_custom_call", output_to_operand_aliasing={{3}: (1, {})} | custom-call | flops 51539607552 | bytes 134217728 | tf_op jit(solution)/shard_map/pallas_call | solution.py:832
  724.8 1.3 copy.13
  726.1 1.4 copy.14
  727.5 8.4 %copy.19 = bf16[1,8,256,2048]{3,2,1,0:T(8,128)(2,1)} copy(bf16[1,8,256,2048]{3,2,1,0:T(8,128)(2,1)} %bitcast.18) | data formatting | bytes 16777216
  (1 shorter events, 0.0 us)
